TPU v7x, 128 devices: a whole 4x4x4 slice. The times are simulated.
128 devices in a mesh: band: 4 (over z_lo, core), facet: 32 (over z_hi, x, y).
Axes of the slice: x: 4, y: 4, z: 4 (z_hi: 2, z_lo: 2; z = z_hi * 2 + z_lo), core: 2. Of those that a mesh axis runs over, the one named last changes fastest.
Arguments:
- coeffs: float32 [4, 32, 256, 256], P('band', 'facet'), may hold values from -6 to 6
- dirty: float32 [16, 32, 256, 256], P('band', 'facet'), may hold values from -6 to 6
- psf: float32 [16, 32, 129, 129], P('band', 'facet'), may hold values from -0.046875 to 0.046875
- band_offset: float32 [16], P('band'), may hold values from -0.5 to 0.5
Outputs:
- gradient: float32 [4, 32, 256, 256], P('band', 'facet')
All inputs are finite; a program needn't handle non-finite values.
Results may differ from a plain program's by a relative error of at most 0.0003.
Values sent between devices are 32-bit elements; how exact they have to be, the bound alone decides.
No kernel may reach another device: no remote copies, remote signals or barrier semaphores. Data moves between devices by JAX's collectives and lax.ppermute only.
A program may use at most 64 MiB of HBM per device.

v0:
```python
import functools
import math

import jax
import jax.numpy as jnp
import ml_dtypes
import numpy as np
from jax import lax
from jax.experimental import pallas as pl
from jax.experimental.pallas import tpu as pltpu
from jax.sharding import PartitionSpec as P

P_SIZE = 256
B = 64
TERMS = 4
FGY = 4
FROWS = 8
FACETS = 32
K = 129
NR = 384
NC = 512
HR = NR // 2
HC = NC // 2
SPAN = P_SIZE + 2 * B
KP = 144

F32 = jnp.float32
BF16 = jnp.bfloat16


def basis(length, coords):
    freq = (np.arange(length // 2) + 0.5) * (2.0 * np.pi / length)
    angle = freq[:, None] * np.asarray(coords, np.float64)[None, :]
    return np.concatenate([np.cos(angle), np.sin(angle)], axis=0)


def halves(matrix):
    high = matrix.astype(np.float32).astype(ml_dtypes.bfloat16)
    low = (matrix - high.astype(np.float64)).astype(np.float32).astype(ml_dtypes.bfloat16)
    return high, low


@functools.cache
def tables():
    coords = np.concatenate([np.arange(P_SIZE + B), np.arange(-B, 0)])
    offsets = np.arange(KP) - B
    fc = basis(NC, coords).T
    fr = basis(NR, coords)
    gc = basis(NC, offsets[:K]).T
    gr = basis(NR, offsets) * (np.arange(KP) < K)[None, :]
    dc = basis(NC, np.arange(P_SIZE)) * (2.0 / NC)
    dr = basis(NR, np.arange(P_SIZE)).T * (2.0 / NR) * 0.5

    def right(m):
        h, l = halves(m)
        return np.concatenate([h, l], axis=0)

    def left(m):
        h, l = halves(m)
        return np.concatenate([h, l], axis=1)

    edge = np.zeros((8, NC), np.float32)
    edge[0] = gc[K - 1]
    return dict(
        fc=right(fc), fr=left(fr), gc=right(gc[:128]), gr=left(gr), dc=right(dc), dr=left(dr), edge=edge
    )


def split(x):
    high = x.astype(BF16)
    return high, (x - high.astype(F32)).astype(BF16)


def dot(a, b):
    return jnp.dot(a, b, preferred_element_type=F32)


def times(x, table):
    high, low = split(x)
    n = table.shape[0] // 2
    return dot(high, table[:n]) + (dot(low, table[:n]) + dot(high, table[n:]))


def under(table, x):
    high, low = split(x)
    n = table.shape[1] // 2
    return dot(table[:, :n], high) + (dot(table[:, :n], low) + dot(table[:, n:], high))


def diagonal(ref, cc, cs, sc, ss):
    ref[0, 0:HR, 0:HC] = cc - ss
    ref[0, HR:NR, 0:HC] = sc + cs
    ref[0, 0:HR, HC:NC] = cc + ss
    ref[0, HR:NR, HC:NC] = sc - cs


VMEM = pl.BlockSpec(memory_space=pltpu.VMEM)
SMEM = pl.BlockSpec(memory_space=pltpu.SMEM)
PARAMS = pltpu.CompilerParams(vmem_limit_bytes=48 * 1024 * 1024)


def shape(*dims, dtype=F32):
    return jax.ShapeDtypeStruct(dims, dtype)


def pack_kernel(odd_ref, x_ref, near_ref, far_ref):
    odd = odd_ref[0] == 1
    lane = lax.broadcasted_iota(jnp.int32, (128, 128), 1)
    left, right = x_ref[:, 0:128], x_ref[:, 128:256]
    left = jnp.where(lane < B, left[0:128], pltpu.roll(left[128:256], B, 1))
    right = jnp.where(lane < B, pltpu.roll(right[128:256], B, 1), right[0:128])
    near_ref[...] = jnp.where(odd, left, right)
    far_ref[...] = jnp.where(odd, right, left)


def pack(odd, x):
    return pl.pallas_call(
        pack_kernel,
        out_shape=(shape(128, 128), shape(128, 128)),
        in_specs=[SMEM, VMEM],
        out_specs=(VMEM, VMEM),
        compiler_params=PARAMS,
        name="pack",
    )(odd, x)


def widen_kernel(odd_ref, rowodd_ref, x_ref, near_ref, far_ref, wide_ref, near_out, far_out):
    odd = odd_ref[0] == 1
    rowodd = rowodd_ref[0] == 1
    lane = lax.broadcasted_iota(jnp.int32, (128, 128), 1)
    near, far = near_ref[...], far_ref[...]
    after = jnp.where(odd, far, near)
    before = jnp.where(odd, near, far)
    wide_ref[:, 0:256] = x_ref[...]
    wide_ref[0:128, 256:384] = jnp.where(lane < B, after, before)
    wide_ref[128:256, 256:384] = jnp.where(lane < B, pltpu.roll(after, B, 1), pltpu.roll(before, B, 1))
    top, bottom = wide_ref[0:B, :], wide_ref[256 - B : 256, :]
    near_out[...] = jnp.where(rowodd, top, bottom)
    far_out[...] = jnp.where(rowodd, bottom, top)


def widen(odd, rowodd, x, near, far):
    return pl.pallas_call(
        widen_kernel,
        out_shape=(shape(P_SIZE, SPAN), shape(B, SPAN), shape(B, SPAN)),
        in_specs=[SMEM, SMEM, VMEM, VMEM, VMEM],
        out_specs=(VMEM, VMEM, VMEM),
        compiler_params=PARAMS,
        name="widen",
    )(odd, rowodd, x, near, far)


def own_kernel(wide_ref, fc_ref, fr_ref, out_ref):
    cols = times(wide_ref[...], fc_ref[...])
    high, low = split(cols)
    fr_h, fr_l = fr_ref[:, 0:P_SIZE], fr_ref[:, NR : NR + P_SIZE]
    out_ref[...] = dot(fr_h, high) + (dot(fr_h, low) + dot(fr_l, high))


def own_rows(wide, fc, fr):
    return pl.pallas_call(
        own_kernel,
        out_shape=shape(NR, NC),
        in_specs=[VMEM] * 3,
        out_specs=VMEM,
        compiler_params=PARAMS,
        name="own_rows",
    )(wide, fc, fr)


def powers(offset, first):
    p = [None, offset]
    for _ in range(5):
        p.append(p[-1] * offset)
    p[0] = jnp.float32(1.0)
    return [
        jnp.where(first == 0, p[j], jnp.where(first == 1, p[j + 1], jnp.where(first == 2, p[j + 2], p[j + 3])))
        for j in range(TERMS)
    ]


def moments_kernel(term_ref, off_ref, offs_ref, psf_ref, psfs_ref, mine_ref, send_ref):
    offsets = [off_ref[b] for b in range(4)] + [offs_ref[b] for b in range(4)]
    kernels = [psf_ref.at[b] for b in range(4)] + [psfs_ref.at[b] for b in range(4)]
    for out_ref, first in ((mine_ref, term_ref[0]), (send_ref, term_ref[1])):
        w = [powers(o, first) for o in offsets]
        out_ref[:, 128:KP, :] = jnp.zeros((TERMS + 1, KP - 128, 128), F32)
        for start in range(0, K, 8):
            rows = min(8, K - start)
            main = [k[start : start + rows, 0:128] for k in kernels]
            edge = [k[start : start + rows, 128:129] for k in kernels]
            lane = lax.broadcasted_iota(jnp.int32, (rows, 128), 1)
            edges = jnp.zeros((rows, 128), F32)
            for j in range(TERMS):
                total, side = main[0] * w[0][j], edge[0] * w[0][j]
                for b in range(1, 8):
                    total = total + main[b] * w[b][j]
                    side = side + edge[b] * w[b][j]
                out_ref[j, start : start + rows, :] = total
                edges = jnp.where(lane == j, jnp.broadcast_to(side, (rows, 128)), edges)
            out_ref[TERMS, start : start + rows, :] = edges


def moments(terms, off, off_s, psf, psf_s):
    return pl.pallas_call(
        moments_kernel,
        out_shape=(shape(TERMS + 1, KP, 128), shape(TERMS + 1, KP, 128)),
        in_specs=[SMEM, SMEM, SMEM, VMEM, VMEM],
        out_specs=(VMEM, VMEM),
        compiler_params=PARAMS,
        name="moments",
    )(terms, off, off_s, psf, psf_s)


def kernels_kernel(mine_ref, got_ref, gc_ref, gr_ref, edge_ref, out_ref):
    side = mine_ref[TERMS] + got_ref[TERMS]
    last = edge_ref[0:1, :]
    q = (mine_ref[0] + got_ref[0])
    j = pl.program_id(0)
    q = mine_ref[j] + got_ref[j]
    lane = lax.broadcasted_iota(jnp.int32, (KP, 128), 1)
    column = jnp.sum(jnp.where(lane == j, side, 0.0), axis=1, keepdims=True)
    cols = times(q, gc_ref[...]) + column * last
    y = under(gr_ref[...], cols)
    diagonal(out_ref, y[0:HR, 0:HC], y[0:HR, HC:NC], y[HR:NR, 0:HC], y[HR:NR, HC:NC])


def kernel_spectra(mine, got, gc, gr, edge):
    return pl.pallas_call(
        kernels_kernel,
        grid=(TERMS,),
        out_shape=shape(TERMS, NR, NC),
        in_specs=[VMEM] * 5,
        out_specs=pl.BlockSpec((1, NR, NC), lambda j: (j, 0, 0)),
        compiler_params=PARAMS,
        name="kernel_spectra",
    )(mine, got, gc, gr, edge)


def dirty_kernel(off_ref, dirty_ref, out_ref):
    d = [dirty_ref[b] for b in range(4)]
    for t in range(TERMS):
        w = []
        for b in range(4):
            v = jnp.float32(1.0)
            for _ in range(t):
                v = v * off_ref[b]
            w.append(v)
        out_ref[t] = (d[0] * w[0] + d[1] * w[1]) + (d[2] * w[2] + d[3] * w[3])


def dirty_sums(off, dirty):
    rows = 64
    return pl.pallas_call(
        dirty_kernel,
        grid=(P_SIZE // rows,),
        out_shape=shape(TERMS, P_SIZE, P_SIZE),
        in_specs=[SMEM, pl.BlockSpec((4, rows, P_SIZE), lambda i: (0, i, 0))],
        out_specs=pl.BlockSpec((TERMS, rows, P_SIZE), lambda i: (0, i, 0)),
        compiler_params=PARAMS,
        name="dirty_sums",
    )(off, dirty)


def product_back(x_ref, y_ref, dirty_ref, dc_ref, dr_ref, z_ref, out_ref):
    a, b = x_ref[0, 0:HR, 0:HC], x_ref[0, HR:NR, 0:HC]
    c, d = y_ref[0, 0:HR, 0:HC], y_ref[0, HR:NR, 0:HC]
    rp, ip = a * c - b * d, a * d + b * c
    a, b = x_ref[0, 0:HR, HC:NC], x_ref[0, HR:NR, HC:NC]
    c, d = y_ref[0, 0:HR, HC:NC], y_ref[0, HR:NR, HC:NC]
    rm, im = a * c - b * d, a * d + b * c
    z_ref[0:HR, 0:HC] = rp + rm
    z_ref[0:HR, HC:NC] = ip - im
    z_ref[HR:NR, 0:HC] = ip + im
    z_ref[HR:NR, HC:NC] = rm - rp
    cols = times(z_ref[...], dc_ref[...])
    out_ref[...] = dirty_ref[0] - under(dr_ref[...], cols)


def first_kernel(idx_ref, own_ref, near_ref, far_ref, fc_ref, fr_ref, dc_ref, dr_ref, y0, y1, d0, d1,
                 x_ref, out0, out1, z_ref):
    rowodd = idx_ref[4] == 1
    near, far = near_ref[...], far_ref[...]
    halo = jnp.concatenate([jnp.where(rowodd, far, near), jnp.where(rowodd, near, far)], axis=0)
    cols = times(halo, fc_ref[...])
    high, low = split(cols)
    fr_h, fr_l = fr_ref[:, P_SIZE:NR], fr_ref[:, NR + P_SIZE :]
    x = own_ref[...] + (dot(fr_h, high) + (dot(fr_h, low) + dot(fr_l, high)))
    diagonal(x_ref, x[0:HR, 0:HC], x[0:HR, HC:NC], x[HR:NR, 0:HC], x[HR:NR, HC:NC])
    product_back(x_ref, y0, d0, dc_ref, dr_ref, z_ref, out0)
    product_back(x_ref, y1, d1, dc_ref, dr_ref, z_ref, out1)


def second_kernel(idx_ref, x_ref, dc_ref, dr_ref, y0, y1, d0, d1, out0, out1, z_ref):
    product_back(x_ref, y0, d0, dc_ref, dr_ref, z_ref, out0)
    product_back(x_ref, y1, d1, dc_ref, dr_ref, z_ref, out1)


def whole(*dims):
    return pl.BlockSpec(dims, lambda i, idx: (0,) * len(dims))


def pick(n, *dims):
    return pl.BlockSpec((1,) + dims, lambda i, idx: (idx[n],) + (0,) * len(dims))


def first(idx, own, near, far, fc, fr, dc, dr, y, dirty):
    return pl.pallas_call(
        first_kernel,
        grid_spec=pltpu.PrefetchScalarGridSpec(
            num_scalar_prefetch=1,
            grid=(1,),
            in_specs=[whole(*v.shape) for v in (own, near, far, fc, fr, dc, dr)]
            + [pick(0, NR, NC), pick(1, NR, NC), pick(0, P_SIZE, P_SIZE), pick(1, P_SIZE, P_SIZE)],
            out_specs=(whole(1, NR, NC), whole(P_SIZE, P_SIZE), whole(P_SIZE, P_SIZE)),
            scratch_shapes=[pltpu.VMEM((NR, NC), F32)],
        ),
        out_shape=(shape(1, NR, NC), shape(P_SIZE, P_SIZE), shape(P_SIZE, P_SIZE)),
        compiler_params=PARAMS,
        name="first",
    )(idx, own, near, far, fc, fr, dc, dr, y, y, dirty, dirty)


def second(idx, x, dc, dr, y, dirty):
    return pl.pallas_call(
        second_kernel,
        grid_spec=pltpu.PrefetchScalarGridSpec(
            num_scalar_prefetch=1,
            grid=(1,),
            in_specs=[whole(*v.shape) for v in (x, dc, dr)]
            + [pick(2, NR, NC), pick(3, NR, NC), pick(2, P_SIZE, P_SIZE), pick(3, P_SIZE, P_SIZE)],
            out_specs=(whole(P_SIZE, P_SIZE), whole(P_SIZE, P_SIZE)),
            scratch_shapes=[pltpu.VMEM((NR, NC), F32)],
        ),
        out_shape=(shape(P_SIZE, P_SIZE), shape(P_SIZE, P_SIZE)),
        compiler_params=PARAMS,
        name="second",
    )(idx, x, dc, dr, y, y, dirty, dirty)


OFFSET = FGY + FGY // 2


def facet_at(row, col):
    return (row * FGY + col - OFFSET) % FACETS


def exchanges():
    near_c, far_c, near_r, far_r = [], [], [], []
    for row in range(FROWS):
        for col in range(FGY):
            here = facet_at(row, col)
            if col + 1 < FGY:
                there = facet_at(row, col + 1)
                (near_c if here % 2 == 0 else far_c).extend([(here, there), (there, here)])
            if row + 1 < FROWS:
                there = facet_at(row + 1, col)
                (near_r if here // FGY % 2 == 0 else far_r).extend([(here, there), (there, here)])
    return near_c, far_c, near_r, far_r


CORES = [(0, 1), (1, 0), (2, 3), (3, 2)]
CHIPS = [(0, 2), (2, 0), (1, 3), (3, 1)]


def body(coeffs, dirty, psf, band_offset):
    table = {k: jnp.asarray(v) for k, v in tables().items()}
    near_c, far_c, near_r, far_r = exchanges()
    band, facet = lax.axis_index("band"), lax.axis_index("facet")
    chip, core = band // 2, band % 2
    other = (1 - chip) * 2
    odd = (facet % 2).reshape(1)
    rowodd = (facet // FGY % 2).reshape(1)
    idx = jnp.stack([other + core, other + 1 - core, band, chip * 2 + 1 - core, rowodd[0]])
    terms = jnp.stack([band, other + core])
    x = coeffs[0, 0]
    psf = psf[:, 0]

    psf_s = lax.ppermute(psf, "band", CORES)
    off_s = lax.ppermute(band_offset, "band", CORES)
    near, far = pack(odd, x)
    far = lax.ppermute(far, "facet", far_c)
    near = lax.ppermute(near, "facet", near_c)
    mine, send = moments(terms, band_offset, off_s, psf, psf_s)
    got = lax.ppermute(send, "band", CHIPS)
    wide, near, far = widen(odd, rowodd, x, near, far)
    far = lax.ppermute(far, "facet", far_r)
    near = lax.ppermute(near, "facet", near_r)
    own = own_rows(wide, table["fc"], table["fr"])
    y = kernel_spectra(mine, got, table["gc"], table["gr"], table["edge"])
    sums = dirty_sums(band_offset, dirty[:, 0])
    spec, same, cross = first(idx, own, near, far, table["fc"], table["fr"], table["dc"], table["dr"], y, sums)
    remote = same + lax.ppermute(cross, "band", CORES)
    remote = lax.ppermute(remote, "band", CHIPS)
    same, cross = second(idx, spec, table["dc"], table["dr"], y, sums)
    cross = lax.ppermute(cross, "band", CORES)
    return ((same + cross) + remote)[None, None]


def solution(mesh):
    placed = (
        P("band", "facet", None, None),
        P("band", "facet", None, None),
        P("band", "facet", None, None),
        P("band"),
    )
    return jax.shard_map(
        body, mesh=mesh, in_specs=placed, out_specs=P("band", "facet", None, None), check_vma=False
    )
```

profile of v0, /device:TPU:24, one launch (start us, length us, event | category | flops | bytes accessed | tf_op | source)
XLA Modules:
  0.0 65.3 jit_solution(18420183589693411141)
XLA Ops:
  0.0 0.0 copy-start.14
  0.0 0.0 copy-start.6
  0.0 0.0 copy-start.5
  0.0 1.2 %copy.16 = f32[4,1,129,129]{3,2,1,0:T(8,128)S(1)} copy(f32[4,1,129,129]{3,1,2,0:T(1,128)} %param.13) | data formatting | bytes 532512
  1.2 0.0 copy-start.1
  1.2 0.0 copy-start.2
  1.2 1.0 %copy.12 = f32[4,129,129]{2,0,1:T(4,128)} copy(f32[4,129,129]{2,1,0:T(8,128)S(1)} %bitcast.13) | data formatting | bytes 532512 | tf_op jit(solution)/shard_map/squeeze | solution.py:377
  2.2 0.0 collective-permute-start.5
  2.3 0.5 collective-permute-start.4
  2.8 0.1 pad_add_fusion.term_ref
  2.8 1.7 %collective-permute-done.5 = f32[4,129,129]{2,0,1:T(4,128)} collective-permute-done((f32[4,129,129]{2,0,1:T(4,128)}, f32[4,129,129]{2,0,1:T(4,128)}, u32[]{:S(2)}, u32[]{:S(2)}) %collective-permute-start.5) | collective-permute-done | bytes 266288 | tf_op jit(solution)/shard_map/ppermute | solution.py:379
  4.5 1.1 %copy.13.psfs_ref = f32[4,129,129]{2,1,0:T(8,128)S(1)} copy(f32[4,129,129]{2,0,1:T(4,128)} %collective-permute-done.5) | data formatting | bytes 532512 | tf_op jit(solution)/shard_map/ppermute | solution.py:379
  5.7 0.0 copy-start.13
  5.7 0.0 collective-permute-done.4.offs_ref
  5.7 0.0 copy-done.14
  5.7 1.9 %moments.1 = (f32[5,144,128]{2,1,0:T(8,128)S(1)}, f32[5,144,128]{2,1,0:T(8,128)}) custom-call(s32[2]{0:T(128)S(1)} %pad_add_fusion.term_ref, f32[4]{0:T(128)S(1)} %copy-done.14, f32[4]{0:T(128)S(1)} %collective-permute-done.4.offs_ref, f32[4,129,129]{2,1,0:T(8,128)S(1)} %bitcast.14, f32[4,129,129]{2,1,0:T(8,128)S(1)} %copy.13.psfs_ref), custom_call_target="tpu_custom_call" | custom-call | tf_op jit(solution)/shard_map/moments/pallas_call | solution.py:205
  7.6 0.0 copy-start.9
  7.6 0.7 %copy-done.9 = f32[5,144,128]{2,1,0:T(8,128)} copy-done((f32[5,144,128]{2,1,0:T(8,128)}, f32[5,144,128]{2,1,0:T(8,128)S(1)}, u32[]{:S(2)}) %copy-start.9) | copy-done | bytes 368664
  8.4 1.9 %collective-permute-start.6 = (f32[5,144,128]{2,1,0:T(8,128)}, f32[5,144,128]{2,1,0:T(8,128)}, u32[]{:S(2)}, u32[]{:S(2)}) collective-permute-start(f32[5,144,128]{2,1,0:T(8,128)} %get-tuple-element.23), channel_id=1, source_target_pairs={{0,64},{64,0},{32,96},{96,32},{1,65},{65,1},{33,97},{97,33},{2,66}... | collective-permute-start | bytes 1105928 | tf_op jit(solution)/shard_map/ppermute | solution.py:385
  10.3 0.0 copy-done.6
  10.3 0.1 pack.1
  10.4 0.8 %collective-permute-start = (f32[128,128]{1,0:T(8,128)S(1)}, f32[128,128]{1,0:T(8,128)S(1)}, u32[]{:S(2)}, u32[]{:S(2)}) collective-permute-start(f32[128,128]{1,0:T(8,128)S(1)} %get-tuple-element.17), channel_id=1, source_target_pairs={{26,27},{27,26},{28,29},{29,28},{30,31},{31,30},{0,1},{1,0},{2,3},... | collective-permute-start | bytes 196616 | tf_op jit(solution)/shard_map/ppermute | solution.py:383
  11.2 3.9 %collective-permute-start.1 = (f32[128,128]{1,0:T(8,128)S(1)}, f32[128,128]{1,0:T(8,128)S(1)}, u32[]{:S(2)}, u32[]{:S(2)}) collective-permute-start(f32[128,128]{1,0:T(8,128)S(1)} %get-tuple-element.18), channel_id=1, source_target_pairs={{27,28},{28,27},{31,0},{0,31},{3,4},{4,3},{7,8},{8,7},{11,12},{12,... | collective-permute-start | bytes 196616 | tf_op jit(solution)/shard_map/ppermute | solution.py:382
  15.1 0.0 collective-permute-done.near_ref
  15.1 4.3 %collective-permute-done.1.far_ref = f32[128,128]{1,0:T(8,128)S(1)} collective-permute-done((f32[128,128]{1,0:T(8,128)S(1)}, f32[128,128]{1,0:T(8,128)S(1)}, u32[]{:S(2)}, u32[]{:S(2)}) %collective-permute-start.1) | collective-permute-done | bytes 65568 | tf_op jit(solution)/shard_map/ppermute | solution.py:382
  19.5 0.8 %widen.1 = (f32[256,384]{1,0:T(8,128)S(1)}, f32[64,384]{1,0:T(8,128)}, f32[64,384]{1,0:T(8,128)}) custom-call(s32[1]{0:T(128)} %bitcast.5.odd_ref, s32[1]{0:T(128)} %bitcast.4.rowodd_ref, f32[256,256]{1,0:T(8,128)S(1)} %bitcast.17, f32[128,128]{1,0:T(8,128)S(1)} %collective-permute-done.near_ref, f32[128,128]{1,0:T(8,128)S(1)} %collective-permute-done.1.far_ref), custom_call_target="tpu_custom_call" | custom-call | tf_op jit(solution)/shard_map/widen/pallas_call | solution.py:143
  20.2 0.0 copy-start.7
  20.2 0.8 %copy-done.7 = f32[256,384]{1,0:T(8,128)} copy-done((f32[256,384]{1,0:T(8,128)}, f32[256,384]{1,0:T(8,128)S(1)}, u32[]{:S(2)}) %copy-start.7) | copy-done | bytes 393240
  21.0 3.4 %collective-permute-start.2 = (f32[64,384]{1,0:T(8,128)}, f32[64,384]{1,0:T(8,128)}, u32[]{:S(2)}, u32[]{:S(2)}) collective-permute-start(f32[64,384]{1,0:T(8,128)} %get-tuple-element.20), channel_id=1, source_target_pairs={{26,30},{30,26},{27,31},{31,27},{0,4},{4,0},{1,5},{5,1},{2,6},{6,2... | collective-permute-start | bytes 294920 | tf_op jit(solution)/shard_map/ppermute | solution.py:388
  24.4 9.8 %collective-permute-start.3 = (f32[64,384]{1,0:T(8,128)}, f32[64,384]{1,0:T(8,128)}, u32[]{:S(2)}, u32[]{:S(2)}) collective-permute-start(f32[64,384]{1,0:T(8,128)} %get-tuple-element.21), channel_id=1, source_target_pairs={{28,0},{0,28},{29,1},{1,29},{30,2},{2,30},{31,3},{3,31},{4,8},{8,4... | collective-permute-start | bytes 294920 | tf_op jit(solution)/shard_map/ppermute | solution.py:387
  34.2 0.0 copy-done.5
  34.2 1.0 %dirty_sums.1.d0.d1 = f32[4,256,256]{2,1,0:T(8,128)S(1)} custom-call(f32[4]{0:T(128)S(1)} %copy-done.14, f32[4,256,256]{2,1,0:T(8,128)S(1)} %bitcast.15), custom_call_target="tpu_custom_call" | custom-call | tf_op jit(solution)/shard_map/dirty_sums/pallas_call | solution.py:254
  35.2 0.1 stack.24.idx_ref
  35.3 0.0 copy-done.1
  35.3 0.0 copy-done.2
  35.3 0.0 copy-start.8
  35.3 1.0 %copy-done.8 = f32[256,384]{1,0:T(8,128)S(1)} copy-done((f32[256,384]{1,0:T(8,128)S(1)}, f32[256,384]{1,0:T(8,128)}, u32[]{:S(2)}) %copy-start.8) | copy-done | bytes 393240
  36.3 0.0 copy-start.3
  36.3 0.0 copy-start.4
  36.3 1.0 %own_rows.1.own_ref = f32[384,512]{1,0:T(8,128)S(1)} custom-call(f32[256,384]{1,0:T(8,128)S(1)} %copy-done.8, bf16[768,512]{1,0:T(8,128)(2,1)S(1)} %copy-done.1, bf16[384,768]{1,0:T(8,128)(2,1)S(1)} %copy-done.2), custom_call_target="tpu_custom_call" | custom-call | tf_op jit(solution)/shard_map/own_rows/pallas_call | solution.py:161
  37.4 0.0 collective-permute-done.6.got_ref
  37.4 0.0 copy-done.13
  37.4 0.0 copy-start.10
  37.4 1.0 %copy-done.10 = f32[5,144,128]{2,1,0:T(8,128)S(1)} copy-done((f32[5,144,128]{2,1,0:T(8,128)S(1)}, f32[5,144,128]{2,1,0:T(8,128)}, u32[]{:S(2)}) %copy-start.10) | copy-done | bytes 368664
  38.4 0.0 copy-start.11
  38.4 1.0 %copy-done.11 = bf16[384,288]{1,0:T(8,128)(2,1)S(1)} copy-done((bf16[384,288]{1,0:T(8,128)(2,1)S(1)}, bf16[384,288]{1,0:T(8,128)(2,1)}, u32[]{:S(2)}) %copy-start.11) | copy-done | bytes 221208
  39.3 0.0 copy-start.12
  39.3 0.9 %copy-done.12 = bf16[256,512]{1,0:T(8,128)(2,1)S(1)} copy-done((bf16[256,512]{1,0:T(8,128)(2,1)S(1)}, bf16[256,512]{1,0:T(8,128)(2,1)}, u32[]{:S(2)}) %copy-start.12) | copy-done | bytes 262168
  40.3 3.8 %kernel_spectra.1.y0.y1 = f32[4,384,512]{2,1,0:T(8,128)S(1)} custom-call(f32[5,144,128]{2,1,0:T(8,128)S(1)} %copy-done.10, f32[5,144,128]{2,1,0:T(8,128)} %collective-permute-done.6.got_ref, bf16[256,512]{1,0:T(8,128)(2,1)S(1)} %copy-done.12, bf16[384,288]{1,0:T(8,128)(2,1)S(1)} %copy-done.11, f32[8,512]{1,0:T(8,128)S(1)} %copy-done.13), custom_call_target="tpu_custom_call" | custom-call | tf_op jit(solution)/shard_map/kernel_spectra/pallas_call | solution.py:229
  44.1 0.0 copy-start
  44.1 1.6 %copy-done = f32[4,384,512]{2,1,0:T(8,128)} copy-done((f32[4,384,512]{2,1,0:T(8,128)}, f32[4,384,512]{2,1,0:T(8,128)S(1)}, u32[]{:S(2)}) %copy-start) | copy-done | bytes 3145752
  45.8 0.0 collective-permute-done.2.near_ref
  45.8 0.0 collective-permute-done.3.far_ref
  45.8 0.0 copy-done.3
  45.8 0.0 copy-done.4
  45.8 5.3 %first.1 = (f32[1,384,512]{2,1,0:T(8,128)S(1)}, f32[256,256]{1,0:T(8,128)S(1)}, f32[256,256]{1,0:T(8,128)S(1)}) custom-call(s32[5]{0:T(128)S(1)} %stack.24.idx_ref, f32[384,512]{1,0:T(8,128)S(1)} %own_rows.1.own_ref, f32[64,384]{1,0:T(8,128)} %collective-permute-done.2.near_ref, f32[64,384]{1,0:T(8,128)} %collective-permute-done.3.far_ref, ...), custom_call_target="tpu_custom_call" | custom-call | tf_op jit(solution)/shard_map/first/pallas_call | solution.py:308
  51.1 0.1 collective-permute-start.8
  51.2 4.4 %second.1 = (f32[256,256]{1,0:T(8,128)S(1)}, f32[256,256]{1,0:T(8,128)S(1)}) custom-call(s32[5]{0:T(128)S(1)} %stack.24.idx_ref, f32[1,384,512]{2,1,0:T(8,128)S(1)} %get-tuple-element.24.x_ref, bf16[1024,256]{1,0:T(8,128)(2,1)S(1)} %copy-done.3, bf16[256,768]{1,0:T(8,128)(2,1)S(1)} %copy-done.4, f32[4,384,512]{2,1,0:T(8,128)} %copy-done, ...), custom_call_target="tpu_custom_call" | custom-call | tf_op jit(solution)/shard_map/second/pallas_call | solution.py:325
  55.6 0.6 collective-permute-start.7
  56.2 0.0 collective-permute-done.8
  56.2 0.1 collective-permute-start.9
  56.3 1.0 %collective-permute-done.7 = f32[256,256]{1,0:T(8,128)S(1)} collective-permute-done((f32[256,256]{1,0:T(8,128)S(1)}, f32[256,256]{1,0:T(8,128)S(1)}, u32[]{:S(2)}, u32[]{:S(2)}) %collective-permute-start.7) | collective-permute-done | bytes 262176 | tf_op jit(solution)/shard_map/ppermute | solution.py:396
  57.3 7.2 %collective-permute-done.9 = f32[256,256]{1,0:T(8,128)S(1)} collective-permute-done((f32[256,256]{1,0:T(8,128)S(1)}, f32[256,256]{1,0:T(8,128)S(1)}, u32[]{:S(2)}, u32[]{:S(2)}) %collective-permute-start.9) | collective-permute-done | bytes 262176 | tf_op jit(solution)/shard_map/ppermute | solution.py:394
  64.5 0.8 %add_bitcast_fusion = f32[1,1,256,256]{3,2,1,0:T(8,128)} fusion(f32[256,256]{1,0:T(8,128)S(1)} %collective-permute-done.9, f32[256,256]{1,0:T(8,128)S(1)} %get-tuple-element.25, f32[256,256]{1,0:T(8,128)S(1)} %collective-permute-done.7), kind=kLoop, calls=%fused_computation.1 | loop fusion | flops 131072 | bytes 1048576 | tf_op jit(solution)/shard_map/broadcast_in_dim | solution.py:397
  (1 shorter events, 0.0 us)
Async XLA Ops:
  0.0 5.7 %copy-start.14 = (f32[4]{0:T(128)S(1)}, f32[4]{0:T(128)}, u32[]{:S(2)}) copy-start(f32[4]{0:T(128)} %off_ref.3) | copy-start | bytes 52
  0.0 10.3 %copy-start.6 = (f32[1,1,256,256]{3,2,1,0:T(8,128)S(1)}, f32[1,1,256,256]{3,2,1,0:T(8,128)}, u32[]{:S(2)}) copy-start(f32[1,1,256,256]{3,2,1,0:T(8,128)} %param.11) | copy-start | bytes 786436
  0.0 34.2 %copy-start.5 = (f32[4,1,256,256]{3,2,1,0:T(8,128)S(1)}, f32[4,1,256,256]{3,2,1,0:T(8,128)}, u32[]{:S(2)}) copy-start(f32[4,1,256,256]{3,2,1,0:T(8,128)} %param.12) | copy-start | bytes 3145732
  1.2 34.1 %copy-start.1 = (bf16[768,512]{1,0:T(8,128)(2,1)S(1)}, bf16[768,512]{1,0:T(8,128)(2,1)}, u32[]{:S(2)}) copy-start(bf16[768,512]{1,0:T(8,128)(2,1)} %constant.66.clone.fc_ref) | copy-start | bytes 2359300
  1.2 34.1 %copy-start.2 = (bf16[384,768]{1,0:T(8,128)(2,1)S(1)}, bf16[384,768]{1,0:T(8,128)(2,1)}, u32[]{:S(2)}) copy-start(bf16[384,768]{1,0:T(8,128)(2,1)} %constant.67.clone.fr_ref) | copy-start | bytes 1769476
  2.2 2.3 %collective-permute-start.5 = (f32[4,129,129]{2,0,1:T(4,128)}, f32[4,129,129]{2,0,1:T(4,128)}, u32[]{:S(2)}, u32[]{:S(2)}) collective-permute-start(f32[4,129,129]{2,0,1:T(4,128)} %copy.12), channel_id=1, source_target_pairs={{0,32},{32,0},{64,96},{96,64},{1,33},{33,1},{65,97},{97,65},{2,34}... | collective-permute-start | bytes 798776 | tf_op jit(solution)/shard_map/ppermute | solution.py:379
  2.3 3.4 %collective-permute-start.4 = (f32[4]{0:T(128)}, f32[4]{0:T(128)S(1)}, u32[]{:S(2)}, u32[]{:S(2)}) collective-permute-start(f32[4]{0:T(128)} %off_ref.3), channel_id=1, source_target_pairs={{0,32},{32,0},{64,96},{96,64},{1,33},{33,1},{65,97},{97,65},{2,34}... | collective-permute-start | bytes 56 | tf_op jit(solution)/shard_map/ppermute | solution.py:380
  5.7 31.7 %copy-start.13 = (f32[8,512]{1,0:T(8,128)S(1)}, f32[8,512]{1,0:T(8,128)}, u32[]{:S(2)}) copy-start(f32[8,512]{1,0:T(8,128)} %constant.72.clone.edge_ref) | copy-start | bytes 49156
  7.6 0.7 %copy-start.9 = (f32[5,144,128]{2,1,0:T(8,128)}, f32[5,144,128]{2,1,0:T(8,128)S(1)}, u32[]{:S(2)}) copy-start(f32[5,144,128]{2,1,0:T(8,128)S(1)} %get-tuple-element.22.mine_ref) | copy-start | bytes 1105924
  8.4 29.0 %collective-permute-start.6 = (f32[5,144,128]{2,1,0:T(8,128)}, f32[5,144,128]{2,1,0:T(8,128)}, u32[]{:S(2)}, u32[]{:S(2)}) collective-permute-start(f32[5,144,128]{2,1,0:T(8,128)} %get-tuple-element.23), channel_id=1, source_target_pairs={{0,64},{64,0},{32,96},{96,32},{1,65},{65,1},{33,97},{97,33},{2,66}... | collective-permute-start | bytes 1105928 | tf_op jit(solution)/shard_map/ppermute | solution.py:385
  10.4 4.7 %collective-permute-start = (f32[128,128]{1,0:T(8,128)S(1)}, f32[128,128]{1,0:T(8,128)S(1)}, u32[]{:S(2)}, u32[]{:S(2)}) collective-permute-start(f32[128,128]{1,0:T(8,128)S(1)} %get-tuple-element.17), channel_id=1, source_target_pairs={{26,27},{27,26},{28,29},{29,28},{30,31},{31,30},{0,1},{1,0},{2,3},... | collective-permute-start | bytes 196616 | tf_op jit(solution)/shard_map/ppermute | solution.py:383
  11.2 8.3 %collective-permute-start.1 = (f32[128,128]{1,0:T(8,128)S(1)}, f32[128,128]{1,0:T(8,128)S(1)}, u32[]{:S(2)}, u32[]{:S(2)}) collective-permute-start(f32[128,128]{1,0:T(8,128)S(1)} %get-tuple-element.18), channel_id=1, source_target_pairs={{27,28},{28,27},{31,0},{0,31},{3,4},{4,3},{7,8},{8,7},{11,12},{12,... | collective-permute-start | bytes 196616 | tf_op jit(solution)/shard_map/ppermute | solution.py:382
  20.2 0.8 %copy-start.7 = (f32[256,384]{1,0:T(8,128)}, f32[256,384]{1,0:T(8,128)S(1)}, u32[]{:S(2)}) copy-start(f32[256,384]{1,0:T(8,128)S(1)} %get-tuple-element.19.wide_ref) | copy-start | bytes 1179652
  21.0 24.8 %collective-permute-start.2 = (f32[64,384]{1,0:T(8,128)}, f32[64,384]{1,0:T(8,128)}, u32[]{:S(2)}, u32[]{:S(2)}) collective-permute-start(f32[64,384]{1,0:T(8,128)} %get-tuple-element.20), channel_id=1, source_target_pairs={{26,30},{30,26},{27,31},{31,27},{0,4},{4,0},{1,5},{5,1},{2,6},{6,2... | collective-permute-start | bytes 294920 | tf_op jit(solution)/shard_map/ppermute | solution.py:388
  24.4 21.4 %collective-permute-start.3 = (f32[64,384]{1,0:T(8,128)}, f32[64,384]{1,0:T(8,128)}, u32[]{:S(2)}, u32[]{:S(2)}) collective-permute-start(f32[64,384]{1,0:T(8,128)} %get-tuple-element.21), channel_id=1, source_target_pairs={{28,0},{0,28},{29,1},{1,29},{30,2},{2,30},{31,3},{3,31},{4,8},{8,4... | collective-permute-start | bytes 294920 | tf_op jit(solution)/shard_map/ppermute | solution.py:387
  35.3 1.0 %copy-start.8 = (f32[256,384]{1,0:T(8,128)S(1)}, f32[256,384]{1,0:T(8,128)}, u32[]{:S(2)}) copy-start(f32[256,384]{1,0:T(8,128)} %copy-done.7) | copy-start | bytes 1179652
  36.3 9.4 %copy-start.3 = (bf16[1024,256]{1,0:T(8,128)(2,1)S(1)}, bf16[1024,256]{1,0:T(8,128)(2,1)}, u32[]{:S(2)}) copy-start(bf16[1024,256]{1,0:T(8,128)(2,1)} %constant.70.clone.dc_ref) | copy-start | bytes 1572868
  36.3 9.4 %copy-start.4 = (bf16[256,768]{1,0:T(8,128)(2,1)S(1)}, bf16[256,768]{1,0:T(8,128)(2,1)}, u32[]{:S(2)}) copy-start(bf16[256,768]{1,0:T(8,128)(2,1)} %constant.71.clone.dr_ref) | copy-start | bytes 1179652
  37.4 1.0 %copy-start.10 = (f32[5,144,128]{2,1,0:T(8,128)S(1)}, f32[5,144,128]{2,1,0:T(8,128)}, u32[]{:S(2)}) copy-start(f32[5,144,128]{2,1,0:T(8,128)} %copy-done.9) | copy-start | bytes 1105924
  38.4 1.0 %copy-start.11 = (bf16[384,288]{1,0:T(8,128)(2,1)S(1)}, bf16[384,288]{1,0:T(8,128)(2,1)}, u32[]{:S(2)}) copy-start(bf16[384,288]{1,0:T(8,128)(2,1)} %constant.69.clone.gr_ref) | copy-start | bytes 663556
  39.3 0.9 %copy-start.12 = (bf16[256,512]{1,0:T(8,128)(2,1)S(1)}, bf16[256,512]{1,0:T(8,128)(2,1)}, u32[]{:S(2)}) copy-start(bf16[256,512]{1,0:T(8,128)(2,1)} %constant.68.clone.gc_ref) | copy-start | bytes 786436
  44.1 1.6 %copy-start = (f32[4,384,512]{2,1,0:T(8,128)}, f32[4,384,512]{2,1,0:T(8,128)S(1)}, u32[]{:S(2)}) copy-start(f32[4,384,512]{2,1,0:T(8,128)S(1)} %kernel_spectra.1.y0.y1) | copy-start | bytes 9437188
  51.1 5.1 %collective-permute-start.8 = (f32[256,256]{1,0:T(8,128)S(1)}, f32[256,256]{1,0:T(8,128)S(1)}, u32[]{:S(2)}, u32[]{:S(2)}) collective-permute-start(f32[256,256]{1,0:T(8,128)S(1)} %get-tuple-element.28), channel_id=1, source_target_pairs={{0,32},{32,0},{64,96},{96,64},{1,33},{33,1},{65,97},{97,65},{2,34}... | collective-permute-start | bytes 786440 | tf_op jit(solution)/shard_map/ppermute | solution.py:393
  55.6 1.7 %collective-permute-start.7 = (f32[256,256]{1,0:T(8,128)S(1)}, f32[256,256]{1,0:T(8,128)S(1)}, u32[]{:S(2)}, u32[]{:S(2)}) collective-permute-start(f32[256,256]{1,0:T(8,128)S(1)} %get-tuple-element.26), channel_id=1, source_target_pairs={{0,32},{32,0},{64,96},{96,64},{1,33},{33,1},{65,97},{97,65},{2,34}... | collective-permute-start | bytes 786440 | tf_op jit(solution)/shard_map/ppermute | solution.py:396
  56.2 8.3 %collective-permute-start.9 = (f32[256,256]{1,0:T(8,128)S(1)}, f32[256,256]{1,0:T(8,128)S(1)}, u32[]{:S(2)}, u32[]{:S(2)}) collective-permute-start(f32[256,256]{1,0:T(8,128)S(1)} %add.38), channel_id=1, source_target_pairs={{0,64},{64,0},{32,96},{96,32},{1,65},{65,1},{33,97},{97,33},{2,66}... | collective-permute-start | bytes 786440 | tf_op jit(solution)/shard_map/ppermute | solution.py:394
where the time goes:
time: 65.7 us; the launch traced here: 65.3 us
  starting transfers between devices  21.1 us (32%)
  Pallas kernels  18.3 us (28%)
  waiting for transfers between devices  14.2 us (22%)
  local copies, waits for them, and re-layouts  10.5 us (16%)
  other arithmetic  0.86 us (1%)
    ppermute x1, starting transfers between devices, body(): far = lax.ppermute(far, 'facet', far_r)  9.82 us
    unnamed x31, local copies, waits for them, and re-layouts  8.24 us
    ppermute x1, waiting for transfers between devices, body(): remote = lax.ppermute(remote, 'band', CHIPS)  7.19 us
    pallas_call x1, Pallas kernels, first(): pl.pallas_call(first_kernel, grid_spec=pltpu.PrefetchScalarGridSpec(num_s...  5.3 us
    pallas_call x1, Pallas kernels, second(): pl.pallas_call(second_kernel, grid_spec=pltpu.PrefetchScalarGridSpec(num_...  4.39 us
    ppermute x1, waiting for transfers between devices, body(): far = lax.ppermute(far, 'facet', far_c)  4.33 us
    ppermute x1, starting transfers between devices, body(): far = lax.ppermute(far, 'facet', far_c)  3.88 us
    pallas_call x1, Pallas kernels, kernel_spectra(): pl.pallas_call(kernels_kernel, grid=(TERMS,), out_shape=shape(TERMS, NR,...  3.85 us
  transfers between devices with their start and end apart: 10, of which 4 were waited for; matrix products, arithmetic and copies ran while one was open for 2% of the time, Pallas kernels for 17%

commit v1 on v0

v1 whole, which is shorter than its diff:
```python
import functools

import jax
import jax.numpy as jnp
import ml_dtypes
import numpy as np
from jax import lax
from jax.experimental import pallas as pl
from jax.experimental.pallas import tpu as pltpu
from jax.sharding import PartitionSpec as P


P_SIZE = 256
B = 64
TERMS = 4
FGY = 4
FROWS = 8
FACETS = 32
K = 129
NR = 384
NC = 512
HR = NR // 2
HC = NC // 2
SPAN = P_SIZE + 2 * B
KP = 144
KW = 136
MOMENTS = 2 * TERMS - 1

F32 = jnp.float32
BF16 = jnp.bfloat16


def basis(length, coords):
    freq = (np.arange(length // 2) + 0.5) * (2.0 * np.pi / length)
    angle = freq[:, None] * np.asarray(coords, np.float64)[None, :]
    return np.concatenate([np.cos(angle), np.sin(angle)], axis=0)


def halves(matrix):
    high = matrix.astype(np.float32).astype(ml_dtypes.bfloat16)
    low = (matrix - high.astype(np.float64)).astype(np.float32).astype(ml_dtypes.bfloat16)
    return high, low


@functools.cache
def tables():
    coords = np.concatenate([np.arange(P_SIZE + B), np.arange(-B, 0)])
    offsets = np.arange(KP) - B
    fc = basis(NC, coords).T
    fr = basis(NR, coords)
    gc = basis(NC, offsets[:K]).T
    gr = basis(NR, offsets) * (np.arange(KP) < K)[None, :]
    dc = basis(NC, np.arange(P_SIZE)) * (2.0 / NC)
    dr = basis(NR, np.arange(P_SIZE)).T * (2.0 / NR) * 0.5

    def right(m):
        h, l = halves(m)
        return np.concatenate([h, l], axis=0)

    def left(m):
        h, l = halves(m)
        return np.concatenate([h, l], axis=1)

    edge = np.zeros((8, NC), np.float32)
    edge[0] = gc[K - 1]
    return dict(
        fc=right(fc), fr=left(fr), gc=right(gc[:128]), gr=left(gr), dc=right(dc), dr=left(dr), edge=edge
    )


def split(x):
    high = x.astype(BF16)
    return high, (x - high.astype(F32)).astype(BF16)


def dot(a, b):
    return jnp.dot(a, b, preferred_element_type=F32)


def times(x, table):
    high, low = split(x)
    n = table.shape[0] // 2
    return dot(
        jnp.concatenate([high, low, high], axis=1),
        jnp.concatenate([table[:n], table[:n], table[n:]], axis=0),
    )


def under(table, x):
    high, low = split(x)
    n = table.shape[1] // 2
    return mix(table[:, :n], table[:, n:], high, low)


def mix(left_high, left_low, high, low):
    return dot(
        jnp.concatenate([left_high, left_high, left_low], axis=1),
        jnp.concatenate([high, low, high], axis=0),
    )


def diagonal(ref, cc, cs, sc, ss):
    ref[0, 0:HR, 0:HC] = cc - ss
    ref[0, HR:NR, 0:HC] = sc + cs
    ref[0, 0:HR, HC:NC] = cc + ss
    ref[0, HR:NR, HC:NC] = sc - cs


VMEM = pl.BlockSpec(memory_space=pltpu.VMEM)
SMEM = pl.BlockSpec(memory_space=pltpu.SMEM)


def grant(mib):
    return pltpu.CompilerParams(vmem_limit_bytes=mib * 1024 * 1024)


def shape(*dims, dtype=F32):
    return jax.ShapeDtypeStruct(dims, dtype)


def pack_kernel(x_ref, near_ref, far_ref):
    odd = lax.axis_index("facet") % 2 == 1
    lane = lax.broadcasted_iota(jnp.int32, (128, 128), 1)
    left, right = x_ref[:, 0:128], x_ref[:, 128:256]
    left = jnp.where(lane < B, left[0:128], pltpu.roll(left[128:256], B, 1))
    right = jnp.where(lane < B, pltpu.roll(right[128:256], B, 1), right[0:128])
    near_ref[...] = jnp.where(odd, left, right)
    far_ref[...] = jnp.where(odd, right, left)


def pack(x):
    return pl.pallas_call(
        pack_kernel,
        out_shape=(shape(128, 128), shape(128, 128)),
        in_specs=[VMEM],
        out_specs=(VMEM, VMEM),
        compiler_params=grant(2),
        name="pack",
    )(x)


def side(near, far, half):
    lane = lax.broadcasted_iota(jnp.int32, near.shape, 1)
    odd = lax.axis_index("facet") % 2 == 1
    after, before = jnp.where(odd, far, near), jnp.where(odd, near, far)
    if half == 0:
        return jnp.where(lane < B, after, before)
    return jnp.where(lane < B, pltpu.roll(after, B, 1), pltpu.roll(before, B, 1))


def edges_kernel(x_ref, near_ref, far_ref, near_out, far_out):
    odd = lax.axis_index("facet") // FGY % 2 == 1
    top = side(near_ref[0:B, :], far_ref[0:B, :], 0)
    bottom = side(near_ref[B:, :], far_ref[B:, :], 1)
    for lanes, above, below in (
        (slice(0, 256), x_ref[0:B, :], x_ref[256 - B : 256, :]),
        (slice(256, 384), top, bottom),
    ):
        near_out[:, lanes] = jnp.where(odd, above, below)
        far_out[:, lanes] = jnp.where(odd, below, above)


def edges(x, near, far):
    return pl.pallas_call(
        edges_kernel,
        out_shape=(shape(B, SPAN), shape(B, SPAN)),
        in_specs=[VMEM] * 3,
        out_specs=(VMEM, VMEM),
        compiler_params=grant(2),
        name="edges",
    )(x, near, far)


def own_kernel(x_ref, near_ref, far_ref, fc_ref, fr_ref, out_ref):
    near, far = near_ref[...], far_ref[...]
    borders = jnp.concatenate([side(near, far, 0), side(near, far, 1)], axis=0)
    cols = times(jnp.concatenate([x_ref[...], borders], axis=1), fc_ref[...])
    high, low = split(cols)
    fr_h, fr_l = fr_ref[:, 0:P_SIZE], fr_ref[:, NR : NR + P_SIZE]
    out_ref[...] = mix(fr_h, fr_l, high, low)


def own_rows(*args):
    return pl.pallas_call(
        own_kernel,
        out_shape=shape(NR, NC),
        in_specs=[VMEM] * 5,
        out_specs=VMEM,
        compiler_params=grant(8),
        name="own_rows",
    )(*args)


def moments_kernel(off_ref, psf_ref, out_ref):
    weights = []
    for b in range(4):
        p = [jnp.float32(1.0)]
        for _ in range(MOMENTS - 1):
            p.append(p[-1] * off_ref[b])
        weights.append(p)
    lane = lax.broadcasted_iota(jnp.int32, (8, 128), 1)
    columns = []
    for start in range(0, 128, 8):
        main = [psf_ref[b, 0, start : start + 8, 0:128] for b in range(4)]
        edge = [psf_ref[b, 0, start : start + 8, 128:129] for b in range(4)]
        packed = jnp.zeros((8, 128), F32)
        for b in range(4):
            packed = jnp.where(lane == b, jnp.broadcast_to(edge[b], (8, 128)), packed)
        columns.append(packed)
        for s in range(MOMENTS):
            total = main[0] * weights[0][s]
            for b in range(1, 4):
                total = total + main[b] * weights[b][s]
            out_ref[s, start : start + 8, :] = total
    turned = jnp.concatenate(columns, axis=0).T
    last = [psf_ref[b, 0, 128:129, 0:128] for b in range(4)]
    corner = [jnp.broadcast_to(psf_ref[b, 0, 128:129, 128:129], (1, 128)) for b in range(4)]
    rest = jnp.zeros((5, 128), F32)
    for s in range(MOMENTS):
        rows = []
        for parts in (last, [turned[b : b + 1, :] for b in range(4)], corner):
            total = parts[0] * weights[0][s]
            for b in range(1, 4):
                total = total + parts[b] * weights[b][s]
            rows.append(total)
        out_ref[s, 128:KW, :] = jnp.concatenate(rows + [rest], axis=0)


def moments(off, psf):
    return pl.pallas_call(
        moments_kernel,
        out_shape=shape(MOMENTS, KW, 128),
        in_specs=[SMEM, VMEM],
        out_specs=VMEM,
        compiler_params=grant(4),
        name="moments",
    )(off, psf)


def terms():
    band = lax.axis_index("band")
    return band, (band + 2) % 4


def combine_kernel(mine_ref, got_ref, keep_ref, send_ref):
    own, other = terms()
    for j in range(TERMS):
        keep_ref[j] = mine_ref[own + j] + got_ref[own + j]
        send_ref[j] = mine_ref[other + j] + got_ref[other + j]


def combine(mine, got):
    return pl.pallas_call(
        combine_kernel,
        out_shape=(shape(TERMS, KW, 128), shape(TERMS, KW, 128)),
        in_specs=[VMEM, VMEM],
        out_specs=(VMEM, VMEM),
        compiler_params=grant(4),
        name="combine",
    )(mine, got)


def kernels_kernel(mine_ref, got_ref, gc_ref, gr_ref, edge_ref, out_ref):
    j = pl.program_id(0)
    q = mine_ref[j] + got_ref[j]
    pad = jnp.zeros((KP - KW, 128), F32)
    last = edge_ref[0:1, :]
    turned = jnp.concatenate([q[K : K + 1, :], jnp.zeros((127, 128), F32)], axis=0).T[:, 0:1]
    column = jnp.concatenate([turned, q[K + 1 : K + 2, 0:1], jnp.zeros((KP - K, 1), F32)], axis=0)
    cols = times(jnp.concatenate([q, pad], axis=0), gc_ref[...]) + column * last
    y = under(gr_ref[...], cols)
    diagonal(out_ref, y[0:HR, 0:HC], y[0:HR, HC:NC], y[HR:NR, 0:HC], y[HR:NR, HC:NC])


def kernel_spectra(*args):
    return pl.pallas_call(
        kernels_kernel,
        grid=(TERMS,),
        out_shape=shape(TERMS, NR, NC),
        in_specs=[VMEM] * 5,
        out_specs=pl.BlockSpec((1, NR, NC), lambda j: (j, 0, 0)),
        compiler_params=grant(12),
        name="kernel_spectra",
    )(*args)


def dirty_kernel(off_ref, dirty_ref, out_ref):
    d = [dirty_ref[b, 0] for b in range(4)]
    for t in range(TERMS):
        w = []
        for b in range(4):
            v = jnp.float32(1.0)
            for _ in range(t):
                v = v * off_ref[b]
            w.append(v)
        out_ref[t] = (d[0] * w[0] + d[1] * w[1]) + (d[2] * w[2] + d[3] * w[3])


def dirty_sums(off, dirty):
    rows = 64
    return pl.pallas_call(
        dirty_kernel,
        grid=(P_SIZE // rows,),
        out_shape=shape(TERMS, P_SIZE, P_SIZE),
        in_specs=[SMEM, pl.BlockSpec((4, 1, rows, P_SIZE), lambda i: (0, 0, i, 0))],
        out_specs=pl.BlockSpec((TERMS, rows, P_SIZE), lambda i: (0, i, 0)),
        compiler_params=grant(4),
        name="dirty_sums",
    )(off, dirty)


def target(chip, core):
    band = lax.axis_index("band")
    return (band // 2 + chip) % 2 * 2 + (band + core) % 2


def product_back(t, x_ref, y_ref, dirty_ref, dc_ref, dr_ref, z_ref):
    a, b = x_ref[0, 0:HR, 0:HC], x_ref[0, HR:NR, 0:HC]
    c, d = y_ref[t, 0:HR, 0:HC], y_ref[t, HR:NR, 0:HC]
    rp, ip = a * c - b * d, a * d + b * c
    a, b = x_ref[0, 0:HR, HC:NC], x_ref[0, HR:NR, HC:NC]
    c, d = y_ref[t, 0:HR, HC:NC], y_ref[t, HR:NR, HC:NC]
    rm, im = a * c - b * d, a * d + b * c
    z_ref[0:HR, 0:HC] = rp + rm
    z_ref[0:HR, HC:NC] = ip - im
    z_ref[HR:NR, 0:HC] = ip + im
    z_ref[HR:NR, HC:NC] = rm - rp
    cols = times(z_ref[...], dc_ref[...])
    return dirty_ref[t] - under(dr_ref[...], cols)


def first_kernel(own_ref, near_ref, far_ref, fc_ref, fr_ref, dc_ref, dr_ref, y_ref, dirty_ref,
                 x_ref, out_ref, z_ref):
    rowodd = lax.axis_index("facet") // FGY % 2 == 1
    near, far = near_ref[...], far_ref[...]
    halo = jnp.concatenate([jnp.where(rowodd, far, near), jnp.where(rowodd, near, far)], axis=0)
    cols = times(halo, fc_ref[...])
    high, low = split(cols)
    fr_h, fr_l = fr_ref[:, P_SIZE:NR], fr_ref[:, NR + P_SIZE :]
    x = own_ref[...] + mix(fr_h, fr_l, high, low)
    diagonal(x_ref, x[0:HR, 0:HC], x[0:HR, HC:NC], x[HR:NR, 0:HC], x[HR:NR, HC:NC])
    out_ref[...] = product_back(target(1, 1), x_ref, y_ref, dirty_ref, dc_ref, dr_ref, z_ref)


def first(*args):
    return pl.pallas_call(
        first_kernel,
        in_specs=[VMEM] * len(args),
        out_specs=(VMEM, VMEM),
        scratch_shapes=[pltpu.VMEM((NR, NC), F32)],
        out_shape=(shape(1, NR, NC), shape(P_SIZE, P_SIZE)),
        compiler_params=grant(12),
        name="first",
    )(*args)


def back_kernel(chip, core, x_ref, y_ref, dirty_ref, dc_ref, dr_ref, out_ref, z_ref):
    out_ref[...] = product_back(target(chip, core), x_ref, y_ref, dirty_ref, dc_ref, dr_ref, z_ref)


def back(chip, core, *args):
    return pl.pallas_call(
        functools.partial(back_kernel, chip, core),
        in_specs=[VMEM] * len(args),
        out_specs=VMEM,
        scratch_shapes=[pltpu.VMEM((NR, NC), F32)],
        out_shape=shape(P_SIZE, P_SIZE),
        compiler_params=grant(12),
    )(*args)


def total_kernel(*refs):
    value = refs[0][...]
    for ref in refs[1:-1]:
        value = value + ref[...]
    refs[-1][...] = value


def total(*args):
    return pl.pallas_call(
        total_kernel,
        out_shape=shape(P_SIZE, P_SIZE),
        in_specs=[VMEM] * len(args),
        out_specs=VMEM,
        compiler_params=grant(4),
    )(*args)


OFFSET = FGY + FGY // 2


def facet_at(row, col):
    return (row * FGY + col - OFFSET) % FACETS


def exchanges():
    near_c, far_c, near_r, far_r = [], [], [], []
    for row in range(FROWS):
        for col in range(FGY):
            here = facet_at(row, col)
            if col + 1 < FGY:
                there = facet_at(row, col + 1)
                (near_c if here % 2 == 0 else far_c).extend([(here, there), (there, here)])
            if row + 1 < FROWS:
                there = facet_at(row + 1, col)
                (near_r if here // FGY % 2 == 0 else far_r).extend([(here, there), (there, here)])
    return near_c, far_c, near_r, far_r


CORES = [(0, 1), (1, 0), (2, 3), (3, 2)]
CHIPS = [(0, 2), (2, 0), (1, 3), (3, 1)]


def body(coeffs, dirty, psf, band_offset):
    table = {k: jnp.asarray(v) for k, v in tables().items()}
    near_c, far_c, near_r, far_r = exchanges()
    x = coeffs[0, 0]
    near, far = pack(x)
    far = lax.ppermute(far, "facet", far_c)
    near = lax.ppermute(near, "facet", near_c)
    mine = moments(band_offset, psf)
    got = lax.ppermute(mine, "band", CORES)
    mine, send = combine(mine, got)
    got = lax.ppermute(send, "band", CHIPS)
    near_row, far_row = edges(x, near, far)
    far_row = lax.ppermute(far_row, "facet", far_r)
    near_row = lax.ppermute(near_row, "facet", near_r)
    own = own_rows(x, near, far, table["fc"], table["fr"])
    y = kernel_spectra(mine, got, table["gc"], table["gr"], table["edge"])
    sums = dirty_sums(band_offset, dirty)
    fixed = (y, sums, table["dc"], table["dr"])
    spec, cross = first(own, near_row, far_row, table["fc"], table["fr"], *fixed[2:], *fixed[:2])
    cross = lax.ppermute(cross, "band", CORES)
    remote = back(1, 0, spec, *fixed)
    remote = total(remote, cross)
    remote = lax.ppermute(remote, "band", CHIPS)
    cross = back(0, 1, spec, *fixed)
    cross = lax.ppermute(cross, "band", CORES)
    same = back(0, 0, spec, *fixed)
    return total(same, cross, remote)[None, None]


def solution(mesh):
    placed = (
        P("band", "facet", None, None),
        P("band", "facet", None, None),
        P("band", "facet", None, None),
        P("band"),
    )
    return jax.shard_map(
        body, mesh=mesh, in_specs=placed, out_specs=P("band", "facet", None, None), check_vma=False
    )
```

time: 65.7 us -> 48.1 us (0.73)
  local copies, waits for them, and re-layouts: 10.5 us -> 1.94 us
  Pallas kernels: 18.3 us -> 11.6 us
  waiting for transfers between devices: 14.2 us -> 13.3 us
  other arithmetic: 0.86 us -> 0 us
    unnamed x31 -> x21, local copies, waits for them, and re-layouts: 8.24 us -> 1.94 us
    pallas_call x5 -> x10, Pallas kernels: 13.4 us -> 7.94 us  [the longest x3 3.35 us: back(): pl.pallas_call(functools.partial(back_kernel, chip, core), in_specs=[VMEM...]
    pallas_call x1, Pallas kernels: 3.85 us -> 2.55 us  [kernel_spectra(): pl.pallas_call(kernels_kernel, grid=(TERMS,), out_shape=shape(TERMS, NR,...]
    ppermute x1 -> x0, local copies, waits for them, and re-layouts: 1.15 us -> none  [body(): psf_s = lax.ppermute(psf, 'band', CORES)]
    ppermute x1 -> x2, waiting for transfers between devices: 1.03 us -> 0.01 us  [body(): cross = lax.ppermute(cross, 'band', CORES)]
    squeeze x1 -> x0, local copies, waits for them, and re-layouts: 1.01 us -> none  [body(): psf = psf[:, 0]]
    broadcast_in_dim x1 -> x0, other arithmetic: 0.75 us -> none  [body(): return (same + cross + remote)[None, None]]
    ppermute x5 -> x3, starting transfers between devices: 13.8 us -> 13.3 us  [the longest x1 9.82 us: body(): far_row = lax.ppermute(far_row, 'facet', far_r)]
  transfers between devices with their start and end apart: 10 -> 9, of which waited for: 4 -> 3; matrix products, arithmetic and copies ran while one was open for 2% -> 0% of each run, Pallas kernels for 17% -> 17%
where the time goes in v1:
time: 48.1 us; the launch traced here: 47.9 us
  starting transfers between devices  20.7 us (43%)
  waiting for transfers between devices  13.3 us (28%)
  Pallas kernels  11.6 us (24%)
  local copies, waits for them, and re-layouts  1.94 us (4%)
    ppermute x1, starting transfers between devices, body(): far_row = lax.ppermute(far_row, 'facet', far_r)  9.82 us
    ppermute x1, waiting for transfers between devices, body(): remote = lax.ppermute(remote, 'band', CHIPS)  7.09 us
    ppermute x1, waiting for transfers between devices, body(): far = lax.ppermute(far, 'facet', far_c)  4.36 us
    ppermute x1, starting transfers between devices, body(): far = lax.ppermute(far, 'facet', far_c)  3.88 us
    ppermute x1, starting transfers between devices, body(): near_row = lax.ppermute(near_row, 'facet', near_r)  3.4 us
    pallas_call x3, Pallas kernels, back(): pl.pallas_call(functools.partial(back_kernel, chip, core), in_specs=[VMEM...  3.35 us
    pallas_call x1, Pallas kernels, kernel_spectra(): pl.pallas_call(kernels_kernel, grid=(TERMS,), out_shape=shape(TERMS, NR,...  2.55 us
    ppermute x1, starting transfers between devices, body(): got = lax.ppermute(send, 'band', CHIPS)  2 us
  transfers between devices with their start and end apart: 9, of which 3 were waited for; matrix products, arithmetic and copies ran while one was open for 0% of the time, Pallas kernels for 17%

profile of v1, /device:TPU:24, one launch (start us, length us, event | category | flops | bytes accessed | tf_op | source)
XLA Modules:
  0.0 47.9 jit_solution(17787528282317645660)
XLA Ops:
  0.0 0.0 copy-start.3
  0.0 0.0 copy-start.2
  0.0 0.0 copy-start.4
  0.0 0.0 copy-start.5
  0.0 1.2 %copy.12.psf_ref = f32[4,1,129,129]{3,2,1,0:T(8,128)S(1)} copy(f32[4,1,129,129]{3,1,2,0:T(1,128)} %param.13) | data formatting | bytes 532512 | tf_op args[2]
  1.3 0.0 copy-start.9
  1.3 0.6 %copy-done.9 = f32[4]{0:T(128)S(1)} copy-done((f32[4]{0:T(128)S(1)}, f32[4]{0:T(128)}, u32[]{:S(2)}) %copy-start.9) | copy-done | bytes 40
  1.9 0.8 %moments.1.mine_ref = f32[7,136,128]{2,1,0:T(8,128)S(1)} custom-call(f32[4]{0:T(128)S(1)} %copy-done.9, f32[4,1,129,129]{3,2,1,0:T(8,128)S(1)} %copy.12.psf_ref), custom_call_target="tpu_custom_call" | custom-call | tf_op jit(solution)/shard_map/moments/pallas_call | solution.py:230
  2.7 0.0 copy-start.6
  2.7 0.0 copy-start.7
  2.7 0.0 copy-start.8
  2.7 0.1 collective-permute-start.4
  2.8 1.8 %collective-permute-done.4.got_ref = f32[7,136,128]{2,1,0:T(8,128)S(1)} collective-permute-done((f32[7,136,128]{2,1,0:T(8,128)S(1)}, f32[7,136,128]{2,1,0:T(8,128)S(1)}, u32[]{:S(2)}, u32[]{:S(2)}) %collective-permute-start.4) | collective-permute-done | bytes 487456 | tf_op jit(solution)/shard_map/ppermute | solution.py:422
  4.7 0.1 combine.1
  4.7 2.0 %collective-permute-start.5 = (f32[4,136,128]{2,1,0:T(8,128)S(1)}, f32[4,136,128]{2,1,0:T(8,128)S(1)}, u32[]{:S(2)}, u32[]{:S(2)}) collective-permute-start(f32[4,136,128]{2,1,0:T(8,128)S(1)} %get-tuple-element.18), channel_id=1, source_target_pairs={{0,64},{64,0},{32,96},{96,32},{1,65},{65,1},{33,97},{97,33},{2,66}... | collective-permute-start | bytes 835592 | tf_op jit(solution)/shard_map/ppermute | solution.py:424
  6.7 0.0 copy-done.4
  6.7 0.1 pack.1
  6.8 0.8 %collective-permute-start = (f32[128,128]{1,0:T(8,128)S(1)}, f32[128,128]{1,0:T(8,128)S(1)}, u32[]{:S(2)}, u32[]{:S(2)}) collective-permute-start(f32[128,128]{1,0:T(8,128)S(1)} %get-tuple-element.13), channel_id=1, source_target_pairs={{26,27},{27,26},{28,29},{29,28},{30,31},{31,30},{0,1},{1,0},{2,3},... | collective-permute-start | bytes 196616 | tf_op jit(solution)/shard_map/ppermute | solution.py:420
  7.7 3.9 %collective-permute-start.1 = (f32[128,128]{1,0:T(8,128)S(1)}, f32[128,128]{1,0:T(8,128)S(1)}, u32[]{:S(2)}, u32[]{:S(2)}) collective-permute-start(f32[128,128]{1,0:T(8,128)S(1)} %get-tuple-element.14), channel_id=1, source_target_pairs={{27,28},{28,27},{31,0},{0,31},{3,4},{4,3},{7,8},{8,7},{11,12},{12,... | collective-permute-start | bytes 196616 | tf_op jit(solution)/shard_map/ppermute | solution.py:419
  11.6 0.0 collective-permute-done.near_ref
  11.6 4.4 %collective-permute-done.1.far_ref = f32[128,128]{1,0:T(8,128)S(1)} collective-permute-done((f32[128,128]{1,0:T(8,128)S(1)}, f32[128,128]{1,0:T(8,128)S(1)}, u32[]{:S(2)}, u32[]{:S(2)}) %collective-permute-start.1) | collective-permute-done | bytes 65568 | tf_op jit(solution)/shard_map/ppermute | solution.py:419
  15.9 0.1 edges.1
  16.0 3.4 %collective-permute-start.2 = (f32[64,384]{1,0:T(8,128)S(1)}, f32[64,384]{1,0:T(8,128)S(1)}, u32[]{:S(2)}, u32[]{:S(2)}) collective-permute-start(f32[64,384]{1,0:T(8,128)S(1)} %get-tuple-element.15), channel_id=1, source_target_pairs={{26,30},{30,26},{27,31},{31,27},{0,4},{4,0},{1,5},{5,1},{2,6},{6,2... | collective-permute-start | bytes 294920 | tf_op jit(solution)/shard_map/ppermute | solution.py:427
  19.4 9.8 %collective-permute-start.3 = (f32[64,384]{1,0:T(8,128)S(1)}, f32[64,384]{1,0:T(8,128)S(1)}, u32[]{:S(2)}, u32[]{:S(2)}) collective-permute-start(f32[64,384]{1,0:T(8,128)S(1)} %get-tuple-element.16), channel_id=1, source_target_pairs={{28,0},{0,28},{29,1},{1,29},{30,2},{2,30},{31,3},{3,31},{4,8},{8,4... | collective-permute-start | bytes 294920 | tf_op jit(solution)/shard_map/ppermute | solution.py:426
  29.3 0.0 copy-done.5
  29.3 1.0 %dirty_sums.1.dirty_ref = f32[4,256,256]{2,1,0:T(8,128)S(1)} custom-call(f32[4]{0:T(128)S(1)} %copy-done.9, f32[4,1,256,256]{3,2,1,0:T(8,128)S(1)} %copy-done.5), custom_call_target="tpu_custom_call" | custom-call | tf_op jit(solution)/shard_map/dirty_sums/pallas_call | solution.py:301
  30.3 0.0 copy-done.3
  30.3 0.0 copy-done.2
  30.3 0.0 copy-start
  30.3 0.0 copy-start.1
  30.3 1.0 %own_rows.1.own_ref = f32[384,512]{1,0:T(8,128)S(1)} custom-call(f32[256,256]{1,0:T(8,128)S(1)} %bitcast.4, f32[128,128]{1,0:T(8,128)S(1)} %collective-permute-done.near_ref, f32[128,128]{1,0:T(8,128)S(1)} %collective-permute-done.1.far_ref, bf16[768,512]{1,0:T(8,128)(2,1)S(1)} %copy-done.2, bf16[384,768]{1,0:T(8,128)(2,1)S(1)} %copy-done.3), custom_call_target="tpu_custom_call" | custom-call | tf_op jit(solution)/shard_map/own_rows/pallas_call | solution.py:184
  31.3 0.0 collective-permute-done.5.got_ref
  31.3 0.0 copy-done.6
  31.3 0.0 copy-done.7
  31.3 0.0 copy-done.8
  31.3 2.6 %kernel_spectra.1.y_ref = f32[4,384,512]{2,1,0:T(8,128)S(1)} custom-call(f32[4,136,128]{2,1,0:T(8,128)S(1)} %get-tuple-element.17.mine_ref, f32[4,136,128]{2,1,0:T(8,128)S(1)} %collective-permute-done.5.got_ref, bf16[256,512]{1,0:T(8,128)(2,1)S(1)} %copy-done.7, bf16[384,288]{1,0:T(8,128)(2,1)S(1)} %copy-done.6, f32[8,512]{1,0:T(8,128)S(1)} %copy-done.8), custom_call_target="tpu_custom_call" | custom-call | tf_op jit(solution)/shard_map/kernel_spectra/pallas_call | solution.py:276
  33.9 0.0 collective-permute-done.2.near_ref
  33.9 0.0 collective-permute-done.3.far_ref
  33.9 0.0 copy-done
  33.9 0.0 copy-done.1
  33.9 1.9 %first.1 = (f32[1,384,512]{2,1,0:T(8,128)S(1)}, f32[256,256]{1,0:T(8,128)S(1)}) custom-call(f32[384,512]{1,0:T(8,128)S(1)} %own_rows.1.own_ref, f32[64,384]{1,0:T(8,128)S(1)} %collective-permute-done.2.near_ref, f32[64,384]{1,0:T(8,128)S(1)} %collective-permute-done.3.far_ref, bf16[768,512]{1,0:T(8,128)(2,1)S(1)} %copy-done.2, ...), custom_call_target="tpu_custom_call" | custom-call | tf_op jit(solution)/shard_map/first/pallas_call | solution.py:346
  35.9 0.1 collective-permute-start.7
  36.0 1.1 %shard_map.111.refs_0_ = f32[256,256]{1,0:T(8,128)S(1)} custom-call(f32[1,384,512]{2,1,0:T(8,128)S(1)} %get-tuple-element.19.x_ref, f32[4,384,512]{2,1,0:T(8,128)S(1)} %kernel_spectra.1.y_ref, f32[4,256,256]{2,1,0:T(8,128)S(1)} %dirty_sums.1.dirty_ref, bf16[1024,256]{1,0:T(8,128)(2,1)S(1)} %copy-done, bf16[256,768]{1,0:T(8,128)(2,1)S(1)} %copy-done.1), custom_call_target="tpu_custom_call" | custom-call | tf_op jit(solution)/shard_map/pallas_call | solution.py:362
  37.1 1.1 %shard_map.110 = f32[256,256]{1,0:T(8,128)S(1)} custom-call(f32[1,384,512]{2,1,0:T(8,128)S(1)} %get-tuple-element.19.x_ref, f32[4,384,512]{2,1,0:T(8,128)S(1)} %kernel_spectra.1.y_ref, f32[4,256,256]{2,1,0:T(8,128)S(1)} %dirty_sums.1.dirty_ref, bf16[1024,256]{1,0:T(8,128)(2,1)S(1)} %copy-done, bf16[256,768]{1,0:T(8,128)(2,1)S(1)} %copy-done.1), custom_call_target="tpu_custom_call" | custom-call | tf_op jit(solution)/shard_map/pallas_call | solution.py:362
  38.2 0.6 %collective-permute-start.6 = (f32[256,256]{1,0:T(8,128)S(1)}, f32[256,256]{1,0:T(8,128)S(1)}, u32[]{:S(2)}, u32[]{:S(2)}) collective-permute-start(f32[256,256]{1,0:T(8,128)S(1)} %shard_map.110), channel_id=1, source_target_pairs={{0,32},{32,0},{64,96},{96,64},{1,33},{33,1},{65,97},{97,65},{2,34}... | collective-permute-start | bytes 786440 | tf_op jit(solution)/shard_map/ppermute | solution.py:438
  38.8 0.0 collective-permute-done.7.refs_1_
  38.8 0.1 collective-permute-start.8
  38.9 1.1 %shard_map.109.refs_0_ = f32[256,256]{1,0:T(8,128)S(1)} custom-call(f32[1,384,512]{2,1,0:T(8,128)S(1)} %get-tuple-element.19.x_ref, f32[4,384,512]{2,1,0:T(8,128)S(1)} %kernel_spectra.1.y_ref, f32[4,256,256]{2,1,0:T(8,128)S(1)} %dirty_sums.1.dirty_ref, bf16[1024,256]{1,0:T(8,128)(2,1)S(1)} %copy-done, bf16[256,768]{1,0:T(8,128)(2,1)S(1)} %copy-done.1), custom_call_target="tpu_custom_call" | custom-call | tf_op jit(solution)/shard_map/pallas_call | solution.py:362
  40.1 0.0 collective-permute-done.6.refs_1_
  40.1 7.1 %collective-permute-done.8.refs_2_ = f32[256,256]{1,0:T(8,128)S(1)} collective-permute-done((f32[256,256]{1,0:T(8,128)S(1)}, f32[256,256]{1,0:T(8,128)S(1)}, u32[]{:S(2)}, u32[]{:S(2)}) %collective-permute-start.8) | collective-permute-done | bytes 262176 | tf_op jit(solution)/shard_map/ppermute | solution.py:436
  47.2 0.7 %shard_map.113 = f32[256,256]{1,0:T(8,128)} custom-call(f32[256,256]{1,0:T(8,128)S(1)} %shard_map.109.refs_0_, f32[256,256]{1,0:T(8,128)S(1)} %collective-permute-done.6.refs_1_, f32[256,256]{1,0:T(8,128)S(1)} %collective-permute-done.8.refs_2_), custom_call_target="tpu_custom_call" | custom-call | tf_op jit(solution)/shard_map/pallas_call | solution.py:380
  (1 shorter events, 0.0 us)
Async XLA Ops:
  0.0 30.3 %copy-start.3 = (bf16[384,768]{1,0:T(8,128)(2,1)S(1)}, bf16[384,768]{1,0:T(8,128)(2,1)}, u32[]{:S(2)}) copy-start(bf16[384,768]{1,0:T(8,128)(2,1)} %constant.15.clone.fr_ref) | copy-start | bytes 1769476
  0.0 30.3 %copy-start.2 = (bf16[768,512]{1,0:T(8,128)(2,1)S(1)}, bf16[768,512]{1,0:T(8,128)(2,1)}, u32[]{:S(2)}) copy-start(bf16[768,512]{1,0:T(8,128)(2,1)} %constant.14.clone.fc_ref) | copy-start | bytes 2359300
  0.0 6.7 %copy-start.4 = (f32[1,1,256,256]{3,2,1,0:T(8,128)S(1)}, f32[1,1,256,256]{3,2,1,0:T(8,128)}, u32[]{:S(2)}) copy-start(f32[1,1,256,256]{3,2,1,0:T(8,128)} %param.11) | copy-start | bytes 786436
  0.0 29.3 %copy-start.5 = (f32[4,1,256,256]{3,2,1,0:T(8,128)S(1)}, f32[4,1,256,256]{3,2,1,0:T(8,128)}, u32[]{:S(2)}) copy-start(f32[4,1,256,256]{3,2,1,0:T(8,128)} %dirty_ref.1) | copy-start | bytes 3145732
  1.3 0.7 %copy-start.9 = (f32[4]{0:T(128)S(1)}, f32[4]{0:T(128)}, u32[]{:S(2)}) copy-start(f32[4]{0:T(128)} %off_ref.3) | copy-start | bytes 52
  2.7 28.6 %copy-start.6 = (bf16[384,288]{1,0:T(8,128)(2,1)S(1)}, bf16[384,288]{1,0:T(8,128)(2,1)}, u32[]{:S(2)}) copy-start(bf16[384,288]{1,0:T(8,128)(2,1)} %constant.17.clone.gr_ref) | copy-start | bytes 663556
  2.7 28.6 %copy-start.7 = (bf16[256,512]{1,0:T(8,128)(2,1)S(1)}, bf16[256,512]{1,0:T(8,128)(2,1)}, u32[]{:S(2)}) copy-start(bf16[256,512]{1,0:T(8,128)(2,1)} %constant.16.clone.gc_ref) | copy-start | bytes 786436
  2.7 28.6 %copy-start.8 = (f32[8,512]{1,0:T(8,128)S(1)}, f32[8,512]{1,0:T(8,128)}, u32[]{:S(2)}) copy-start(f32[8,512]{1,0:T(8,128)} %constant.20.clone.edge_ref) | copy-start | bytes 49156
  2.7 1.9 %collective-permute-start.4 = (f32[7,136,128]{2,1,0:T(8,128)S(1)}, f32[7,136,128]{2,1,0:T(8,128)S(1)}, u32[]{:S(2)}, u32[]{:S(2)}) collective-permute-start(f32[7,136,128]{2,1,0:T(8,128)S(1)} %moments.1.mine_ref), channel_id=1, source_target_pairs={{0,32},{32,0},{64,96},{96,64},{1,33},{33,1},{65,97},{97,65},{2,34}... | collective-permute-start | bytes 1462280 | tf_op jit(solution)/shard_map/ppermute | solution.py:422
  4.7 26.6 %collective-permute-start.5 = (f32[4,136,128]{2,1,0:T(8,128)S(1)}, f32[4,136,128]{2,1,0:T(8,128)S(1)}, u32[]{:S(2)}, u32[]{:S(2)}) collective-permute-start(f32[4,136,128]{2,1,0:T(8,128)S(1)} %get-tuple-element.18), channel_id=1, source_target_pairs={{0,64},{64,0},{32,96},{96,32},{1,65},{65,1},{33,97},{97,33},{2,66}... | collective-permute-start | bytes 835592 | tf_op jit(solution)/shard_map/ppermute | solution.py:424
  6.8 4.7 %collective-permute-start = (f32[128,128]{1,0:T(8,128)S(1)}, f32[128,128]{1,0:T(8,128)S(1)}, u32[]{:S(2)}, u32[]{:S(2)}) collective-permute-start(f32[128,128]{1,0:T(8,128)S(1)} %get-tuple-element.13), channel_id=1, source_target_pairs={{26,27},{27,26},{28,29},{29,28},{30,31},{31,30},{0,1},{1,0},{2,3},... | collective-permute-start | bytes 196616 | tf_op jit(solution)/shard_map/ppermute | solution.py:420
  7.7 8.3 %collective-permute-start.1 = (f32[128,128]{1,0:T(8,128)S(1)}, f32[128,128]{1,0:T(8,128)S(1)}, u32[]{:S(2)}, u32[]{:S(2)}) collective-permute-start(f32[128,128]{1,0:T(8,128)S(1)} %get-tuple-element.14), channel_id=1, source_target_pairs={{27,28},{28,27},{31,0},{0,31},{3,4},{4,3},{7,8},{8,7},{11,12},{12,... | collective-permute-start | bytes 196616 | tf_op jit(solution)/shard_map/ppermute | solution.py:419
  16.0 17.9 %collective-permute-start.2 = (f32[64,384]{1,0:T(8,128)S(1)}, f32[64,384]{1,0:T(8,128)S(1)}, u32[]{:S(2)}, u32[]{:S(2)}) collective-permute-start(f32[64,384]{1,0:T(8,128)S(1)} %get-tuple-element.15), channel_id=1, source_target_pairs={{26,30},{30,26},{27,31},{31,27},{0,4},{4,0},{1,5},{5,1},{2,6},{6,2... | collective-permute-start | bytes 294920 | tf_op jit(solution)/shard_map/ppermute | solution.py:427
  19.4 14.5 %collective-permute-start.3 = (f32[64,384]{1,0:T(8,128)S(1)}, f32[64,384]{1,0:T(8,128)S(1)}, u32[]{:S(2)}, u32[]{:S(2)}) collective-permute-start(f32[64,384]{1,0:T(8,128)S(1)} %get-tuple-element.16), channel_id=1, source_target_pairs={{28,0},{0,28},{29,1},{1,29},{30,2},{2,30},{31,3},{3,31},{4,8},{8,4... | collective-permute-start | bytes 294920 | tf_op jit(solution)/shard_map/ppermute | solution.py:426
  30.3 3.6 %copy-start = (bf16[1024,256]{1,0:T(8,128)(2,1)S(1)}, bf16[1024,256]{1,0:T(8,128)(2,1)}, u32[]{:S(2)}) copy-start(bf16[1024,256]{1,0:T(8,128)(2,1)} %constant.18.clone.dc_ref) | copy-start | bytes 1572868
  30.3 3.6 %copy-start.1 = (bf16[256,768]{1,0:T(8,128)(2,1)S(1)}, bf16[256,768]{1,0:T(8,128)(2,1)}, u32[]{:S(2)}) copy-start(bf16[256,768]{1,0:T(8,128)(2,1)} %constant.19.clone.dr_ref) | copy-start | bytes 1179652
  35.9 2.9 %collective-permute-start.7 = (f32[256,256]{1,0:T(8,128)S(1)}, f32[256,256]{1,0:T(8,128)S(1)}, u32[]{:S(2)}, u32[]{:S(2)}) collective-permute-start(f32[256,256]{1,0:T(8,128)S(1)} %get-tuple-element.20), channel_id=1, source_target_pairs={{0,32},{32,0},{64,96},{96,64},{1,33},{33,1},{65,97},{97,65},{2,34}... | collective-permute-start | bytes 786440 | tf_op jit(solution)/shard_map/ppermute | solution.py:433
  38.2 1.8 %collective-permute-start.6 = (f32[256,256]{1,0:T(8,128)S(1)}, f32[256,256]{1,0:T(8,128)S(1)}, u32[]{:S(2)}, u32[]{:S(2)}) collective-permute-start(f32[256,256]{1,0:T(8,128)S(1)} %shard_map.110), channel_id=1, source_target_pairs={{0,32},{32,0},{64,96},{96,64},{1,33},{33,1},{65,97},{97,65},{2,34}... | collective-permute-start | bytes 786440 | tf_op jit(solution)/shard_map/ppermute | solution.py:438
  38.8 8.3 %collective-permute-start.8 = (f32[256,256]{1,0:T(8,128)S(1)}, f32[256,256]{1,0:T(8,128)S(1)}, u32[]{:S(2)}, u32[]{:S(2)}) collective-permute-start(f32[256,256]{1,0:T(8,128)S(1)} %shard_map.112), channel_id=1, source_target_pairs={{0,64},{64,0},{32,96},{96,32},{1,65},{65,1},{33,97},{97,33},{2,66}... | collective-permute-start | bytes 786440 | tf_op jit(solution)/shard_map/ppermute | solution.py:436

commit v2 on v1

--- a/solution.py
+++ b/solution.py
@@ -25,6 +25,7 @@
 KP = 144
 KW = 136
 MOMENTS = 2 * TERMS - 1
+DIRTY_PARTS = 4
 
 F32 = jnp.float32
 BF16 = jnp.bfloat16
@@ -108,6 +109,11 @@
 
 VMEM = pl.BlockSpec(memory_space=pltpu.VMEM)
 SMEM = pl.BlockSpec(memory_space=pltpu.SMEM)
+HBM = pl.BlockSpec(memory_space=pltpu.HBM)
+
+
+def in_hbm(x):
+    return pltpu.with_memory_space_constraint(x, pltpu.HBM)
 
 
 def grant(mib):
@@ -118,7 +124,10 @@
     return jax.ShapeDtypeStruct(dims, dtype)
 
 
-def pack_kernel(x_ref, near_ref, far_ref):
+def pack_kernel(x_hbm, x_ref, near_ref, far_ref, sem):
+    copy = pltpu.make_async_copy(x_hbm, x_ref, sem)
+    copy.start()
+    copy.wait()
     odd = lax.axis_index("facet") % 2 == 1
     lane = lax.broadcasted_iota(jnp.int32, (128, 128), 1)
     left, right = x_ref[:, 0:128], x_ref[:, 128:256]
@@ -131,9 +140,10 @@
 def pack(x):
     return pl.pallas_call(
         pack_kernel,
-        out_shape=(shape(128, 128), shape(128, 128)),
-        in_specs=[VMEM],
-        out_specs=(VMEM, VMEM),
+        out_shape=(shape(P_SIZE, P_SIZE), shape(128, 128), shape(128, 128)),
+        in_specs=[HBM],
+        out_specs=(VMEM, VMEM, VMEM),
+        scratch_shapes=[pltpu.SemaphoreType.DMA],
         compiler_params=grant(2),
         name="pack",
     )(x)
@@ -191,7 +201,13 @@
     )(*args)
 
 
-def moments_kernel(off_ref, psf_ref, out_ref):
+def moments_kernel(off_hbm, psf_hbm, out_ref, off_ref, psf_ref, sems):
+    copies = [pltpu.make_async_copy(psf_hbm.at[b, :, 0, :], psf_ref.at[b], sems.at[b]) for b in range(4)]
+    copies.append(pltpu.make_async_copy(off_hbm, off_ref, sems.at[4]))
+    for copy in copies:
+        copy.start()
+    for copy in copies:
+        copy.wait()
     weights = []
     for b in range(4):
         p = [jnp.float32(1.0)]
@@ -201,8 +217,8 @@
     lane = lax.broadcasted_iota(jnp.int32, (8, 128), 1)
     columns = []
     for start in range(0, 128, 8):
-        main = [psf_ref[b, 0, start : start + 8, 0:128] for b in range(4)]
-        edge = [psf_ref[b, 0, start : start + 8, 128:129] for b in range(4)]
+        main = [psf_ref[b, start : start + 8, 0:128] for b in range(4)]
+        edge = [psf_ref[b, start : start + 8, 128:129] for b in range(4)]
         packed = jnp.zeros((8, 128), F32)
         for b in range(4):
             packed = jnp.where(lane == b, jnp.broadcast_to(edge[b], (8, 128)), packed)
@@ -213,8 +229,8 @@
                 total = total + main[b] * weights[b][s]
             out_ref[s, start : start + 8, :] = total
     turned = jnp.concatenate(columns, axis=0).T
-    last = [psf_ref[b, 0, 128:129, 0:128] for b in range(4)]
-    corner = [jnp.broadcast_to(psf_ref[b, 0, 128:129, 128:129], (1, 128)) for b in range(4)]
+    last = [psf_ref[b, 128:129, 0:128] for b in range(4)]
+    corner = [jnp.broadcast_to(psf_ref[b, 128:129, 128:129], (1, 128)) for b in range(4)]
     rest = jnp.zeros((5, 128), F32)
     for s in range(MOMENTS):
         rows = []
@@ -230,11 +246,16 @@
     return pl.pallas_call(
         moments_kernel,
         out_shape=shape(MOMENTS, KW, 128),
-        in_specs=[SMEM, VMEM],
+        in_specs=[HBM, HBM],
         out_specs=VMEM,
+        scratch_shapes=[
+            pltpu.SMEM((4,), F32),
+            pltpu.VMEM((4, K, K), F32),
+            pltpu.SemaphoreType.DMA((5,)),
+        ],
         compiler_params=grant(4),
         name="moments",
-    )(off, psf)
+    )(in_hbm(off), in_hbm(jnp.transpose(psf, (0, 2, 1, 3))))
 
 
 def terms():
@@ -284,29 +305,45 @@
     )(*args)
 
 
-def dirty_kernel(off_ref, dirty_ref, out_ref):
-    d = [dirty_ref[b, 0] for b in range(4)]
-    for t in range(TERMS):
-        w = []
-        for b in range(4):
-            v = jnp.float32(1.0)
-            for _ in range(t):
-                v = v * off_ref[b]
-            w.append(v)
-        out_ref[t] = (d[0] * w[0] + d[1] * w[1]) + (d[2] * w[2] + d[3] * w[3])
+def dirty_kernel(off_hbm, dirty_hbm, out_ref, off_ref, dirty_ref, sems):
+    copies = [pltpu.make_async_copy(off_hbm, off_ref, sems.at[DIRTY_PARTS])]
+    rows = P_SIZE // DIRTY_PARTS
+    for i in range(DIRTY_PARTS):
+        part = pl.ds(i * rows, rows)
+        copies.append(pltpu.make_async_copy(dirty_hbm.at[:, 0, part], dirty_ref.at[:, part], sems.at[i]))
+    for copy in copies:
+        copy.start()
+    copies[0].wait()
+    w = []
+    for b in range(4):
+        p = [jnp.float32(1.0)]
+        for _ in range(TERMS - 1):
+            p.append(p[-1] * off_ref[b])
+        w.append(p)
+    for i in range(DIRTY_PARTS):
+        copies[i + 1].wait()
+        for start in range(i * rows, (i + 1) * rows, 8):
+            d = [dirty_ref[b, start : start + 8, :] for b in range(4)]
+            for t in range(TERMS):
+                out_ref[t, start : start + 8, :] = (d[0] * w[0][t] + d[1] * w[1][t]) + (
+                    d[2] * w[2][t] + d[3] * w[3][t]
+                )
 
 
 def dirty_sums(off, dirty):
-    rows = 64
     return pl.pallas_call(
         dirty_kernel,
-        grid=(P_SIZE // rows,),
         out_shape=shape(TERMS, P_SIZE, P_SIZE),
-        in_specs=[SMEM, pl.BlockSpec((4, 1, rows, P_SIZE), lambda i: (0, 0, i, 0))],
-        out_specs=pl.BlockSpec((TERMS, rows, P_SIZE), lambda i: (0, i, 0)),
+        in_specs=[HBM, HBM],
+        out_specs=VMEM,
+        scratch_shapes=[
+            pltpu.SMEM((4,), F32),
+            pltpu.VMEM((4, P_SIZE, P_SIZE), F32),
+            pltpu.SemaphoreType.DMA((DIRTY_PARTS + 1,)),
+        ],
         compiler_params=grant(4),
         name="dirty_sums",
-    )(off, dirty)
+    )(in_hbm(off), in_hbm(dirty))
 
 
 def target(chip, core):
@@ -414,8 +451,7 @@
 def body(coeffs, dirty, psf, band_offset):
     table = {k: jnp.asarray(v) for k, v in tables().items()}
     near_c, far_c, near_r, far_r = exchanges()
-    x = coeffs[0, 0]
-    near, far = pack(x)
+    x, near, far = pack(in_hbm(coeffs[0, 0]))
     far = lax.ppermute(far, "facet", far_c)
     near = lax.ppermute(near, "facet", near_c)
     mine = moments(band_offset, psf)

time: 48.1 us -> 48.3 us (level)
  Pallas kernels: 11.6 us -> 13.6 us
  local copies, waits for them, and re-layouts: 1.94 us -> 0.04 us
    unnamed x21 -> x14, local copies, waits for them, and re-layouts: 1.94 us -> 0.04 us
    pallas_call x2, Pallas kernels: 1.11 us -> 2.35 us  [the longest x1 1.29 us: dirty_sums(): pl.pallas_call(dirty_kernel, out_shape=shape(TERMS, P_SIZE, P_SIZE), in_s...]
    pallas_call x1, Pallas kernels: 0.77 us -> 1.54 us  [moments(): pl.pallas_call(moments_kernel, out_shape=shape(MOMENTS, KW, 128), in_spec...]
  transfers between devices with their start and end apart: 9 -> 9, of which waited for: 3 -> 3; matrix products, arithmetic and copies ran while one was open for 0% -> 0% of each run, Pallas kernels for 17% -> 19%
where the time goes in v2:
time: 48.3 us; the launch traced here: 48 us
  starting transfers between devices  20.7 us (43%)
  Pallas kernels  13.6 us (28%)
  waiting for transfers between devices  13.3 us (28%)
    ppermute x1, starting transfers between devices, body(): far_row = lax.ppermute(far_row, 'facet', far_r)  9.82 us
    ppermute x1, waiting for transfers between devices, body(): remote = lax.ppermute(remote, 'band', CHIPS)  7.09 us
    ppermute x1, waiting for transfers between devices, body(): far = lax.ppermute(far, 'facet', far_c)  4.36 us
    ppermute x1, starting transfers between devices, body(): far = lax.ppermute(far, 'facet', far_c)  3.88 us
    ppermute x1, starting transfers between devices, body(): near_row = lax.ppermute(near_row, 'facet', near_r)  3.4 us
    pallas_call x3, Pallas kernels, back(): pl.pallas_call(functools.partial(back_kernel, chip, core), in_specs=[VMEM...  3.35 us
    pallas_call x1, Pallas kernels, kernel_spectra(): pl.pallas_call(kernels_kernel, grid=(TERMS,), out_shape=shape(TERMS, NR,...  2.55 us
    ppermute x1, starting transfers between devices, body(): got = lax.ppermute(send, 'band', CHIPS)  2 us
  transfers between devices with their start and end apart: 9, of which 3 were waited for; matrix products, arithmetic and copies ran while one was open for 0% of the time, Pallas kernels for 19%

profile of v2, /device:TPU:24, one launch (start us, length us, event | category | flops | bytes accessed | tf_op | source)
XLA Modules:
  0.0 48.0 jit_solution(15020445243912603794)
XLA Ops:
  0.0 0.0 copy-start.3
  0.0 0.0 copy-start.2
  0.0 1.5 %moments.1.mine_ref = f32[7,136,128]{2,1,0:T(8,128)S(1)} custom-call(f32[4]{0:T(128)} %off_hbm.3, f32[4,129,1,129]{3,2,1,0:T(1,128)} %bitcast.3), custom_call_target="tpu_custom_call" | custom-call | tf_op jit(solution)/shard_map/moments/pallas_call | solution.py:246
  1.6 0.0 copy-start.4
  1.6 0.0 copy-start.5
  1.6 0.0 copy-start.6
  1.6 0.1 collective-permute-start.4
  1.7 1.8 %collective-permute-done.4.got_ref = f32[7,136,128]{2,1,0:T(8,128)S(1)} collective-permute-done((f32[7,136,128]{2,1,0:T(8,128)S(1)}, f32[7,136,128]{2,1,0:T(8,128)S(1)}, u32[]{:S(2)}, u32[]{:S(2)}) %collective-permute-start.4) | collective-permute-done | bytes 487456 | tf_op jit(solution)/shard_map/ppermute | solution.py:458
  3.5 0.1 combine.1
  3.6 2.0 %collective-permute-start.5 = (f32[4,136,128]{2,1,0:T(8,128)S(1)}, f32[4,136,128]{2,1,0:T(8,128)S(1)}, u32[]{:S(2)}, u32[]{:S(2)}) collective-permute-start(f32[4,136,128]{2,1,0:T(8,128)S(1)} %get-tuple-element.20), channel_id=1, source_target_pairs={{0,64},{64,0},{32,96},{96,32},{1,65},{65,1},{33,97},{97,33},{2,66}... | collective-permute-start | bytes 835592 | tf_op jit(solution)/shard_map/ppermute | solution.py:460
  5.6 1.1 %pack.1 = (f32[256,256]{1,0:T(8,128)S(1)}, f32[128,128]{1,0:T(8,128)S(1)}, f32[128,128]{1,0:T(8,128)S(1)}) custom-call(f32[256,256]{1,0:T(8,128)} %bitcast.4), custom_call_target="tpu_custom_call" | custom-call | tf_op jit(solution)/shard_map/pack/pallas_call | solution.py:141
  6.7 0.8 %collective-permute-start = (f32[128,128]{1,0:T(8,128)S(1)}, f32[128,128]{1,0:T(8,128)S(1)}, u32[]{:S(2)}, u32[]{:S(2)}) collective-permute-start(f32[128,128]{1,0:T(8,128)S(1)} %get-tuple-element.15), channel_id=1, source_target_pairs={{26,27},{27,26},{28,29},{29,28},{30,31},{31,30},{0,1},{1,0},{2,3},... | collective-permute-start | bytes 196616 | tf_op jit(solution)/shard_map/ppermute | solution.py:456
  7.5 3.9 %collective-permute-start.1 = (f32[128,128]{1,0:T(8,128)S(1)}, f32[128,128]{1,0:T(8,128)S(1)}, u32[]{:S(2)}, u32[]{:S(2)}) collective-permute-start(f32[128,128]{1,0:T(8,128)S(1)} %get-tuple-element.16), channel_id=1, source_target_pairs={{27,28},{28,27},{31,0},{0,31},{3,4},{4,3},{7,8},{8,7},{11,12},{12,... | collective-permute-start | bytes 196616 | tf_op jit(solution)/shard_map/ppermute | solution.py:455
  11.4 0.0 collective-permute-done.near_ref
  11.4 4.4 %collective-permute-done.1.far_ref = f32[128,128]{1,0:T(8,128)S(1)} collective-permute-done((f32[128,128]{1,0:T(8,128)S(1)}, f32[128,128]{1,0:T(8,128)S(1)}, u32[]{:S(2)}, u32[]{:S(2)}) %collective-permute-start.1) | collective-permute-done | bytes 65568 | tf_op jit(solution)/shard_map/ppermute | solution.py:455
  15.7 0.1 edges.1
  15.8 3.4 %collective-permute-start.2 = (f32[64,384]{1,0:T(8,128)S(1)}, f32[64,384]{1,0:T(8,128)S(1)}, u32[]{:S(2)}, u32[]{:S(2)}) collective-permute-start(f32[64,384]{1,0:T(8,128)S(1)} %get-tuple-element.17), channel_id=1, source_target_pairs={{26,30},{30,26},{27,31},{31,27},{0,4},{4,0},{1,5},{5,1},{2,6},{6,2... | collective-permute-start | bytes 294920 | tf_op jit(solution)/shard_map/ppermute | solution.py:463
  19.3 9.8 %collective-permute-start.3 = (f32[64,384]{1,0:T(8,128)S(1)}, f32[64,384]{1,0:T(8,128)S(1)}, u32[]{:S(2)}, u32[]{:S(2)}) collective-permute-start(f32[64,384]{1,0:T(8,128)S(1)} %get-tuple-element.18), channel_id=1, source_target_pairs={{28,0},{0,28},{29,1},{1,29},{30,2},{2,30},{31,3},{3,31},{4,8},{8,4... | collective-permute-start | bytes 294920 | tf_op jit(solution)/shard_map/ppermute | solution.py:462
  29.1 1.3 %dirty_sums.1.dirty_ref = f32[4,256,256]{2,1,0:T(8,128)S(1)} custom-call(f32[4]{0:T(128)} %off_hbm.3, f32[4,1,256,256]{3,2,1,0:T(8,128)} %dirty_hbm.1), custom_call_target="tpu_custom_call" | custom-call | tf_op jit(solution)/shard_map/dirty_sums/pallas_call | solution.py:334
  30.4 0.0 copy-done.3
  30.4 0.0 copy-done.2
  30.4 0.0 copy-start
  30.4 0.0 copy-start.1
  30.4 1.0 %own_rows.1.own_ref = f32[384,512]{1,0:T(8,128)S(1)} custom-call(f32[256,256]{1,0:T(8,128)S(1)} %get-tuple-element.14.x_ref, f32[128,128]{1,0:T(8,128)S(1)} %collective-permute-done.near_ref, f32[128,128]{1,0:T(8,128)S(1)} %collective-permute-done.1.far_ref, bf16[768,512]{1,0:T(8,128)(2,1)S(1)} %copy-done.2, bf16[384,768]{1,0:T(8,128)(2,1)S(1)} %copy-done.3), custom_call_target="tpu_custom_call" | custom-call | tf_op jit(solution)/shard_map/own_rows/pallas_call | solution.py:194
  31.4 0.0 collective-permute-done.5.got_ref
  31.4 0.0 copy-done.4
  31.4 0.0 copy-done.5
  31.4 0.0 copy-done.6
  31.4 2.6 %kernel_spectra.1.y_ref = f32[4,384,512]{2,1,0:T(8,128)S(1)} custom-call(f32[4,136,128]{2,1,0:T(8,128)S(1)} %get-tuple-element.19.mine_ref, f32[4,136,128]{2,1,0:T(8,128)S(1)} %collective-permute-done.5.got_ref, bf16[256,512]{1,0:T(8,128)(2,1)S(1)} %copy-done.5, bf16[384,288]{1,0:T(8,128)(2,1)S(1)} %copy-done.4, f32[8,512]{1,0:T(8,128)S(1)} %copy-done.6), custom_call_target="tpu_custom_call" | custom-call | tf_op jit(solution)/shard_map/kernel_spectra/pallas_call | solution.py:297
  34.0 0.0 collective-permute-done.2.near_ref
  34.0 0.0 collective-permute-done.3.far_ref
  34.0 0.0 copy-done
  34.0 0.0 copy-done.1
  34.0 1.9 %first.1 = (f32[1,384,512]{2,1,0:T(8,128)S(1)}, f32[256,256]{1,0:T(8,128)S(1)}) custom-call(f32[384,512]{1,0:T(8,128)S(1)} %own_rows.1.own_ref, f32[64,384]{1,0:T(8,128)S(1)} %collective-permute-done.2.near_ref, f32[64,384]{1,0:T(8,128)S(1)} %collective-permute-done.3.far_ref, bf16[768,512]{1,0:T(8,128)(2,1)S(1)} %copy-done.2, ...), custom_call_target="tpu_custom_call" | custom-call | tf_op jit(solution)/shard_map/first/pallas_call | solution.py:383
  36.0 0.1 collective-permute-start.7
  36.1 1.1 %shard_map.111.refs_0_ = f32[256,256]{1,0:T(8,128)S(1)} custom-call(f32[1,384,512]{2,1,0:T(8,128)S(1)} %get-tuple-element.21.x_ref, f32[4,384,512]{2,1,0:T(8,128)S(1)} %kernel_spectra.1.y_ref, f32[4,256,256]{2,1,0:T(8,128)S(1)} %dirty_sums.1.dirty_ref, bf16[1024,256]{1,0:T(8,128)(2,1)S(1)} %copy-done, bf16[256,768]{1,0:T(8,128)(2,1)S(1)} %copy-done.1), custom_call_target="tpu_custom_call" | custom-call | tf_op jit(solution)/shard_map/pallas_call | solution.py:399
  37.2 1.1 %shard_map.110 = f32[256,256]{1,0:T(8,128)S(1)} custom-call(f32[1,384,512]{2,1,0:T(8,128)S(1)} %get-tuple-element.21.x_ref, f32[4,384,512]{2,1,0:T(8,128)S(1)} %kernel_spectra.1.y_ref, f32[4,256,256]{2,1,0:T(8,128)S(1)} %dirty_sums.1.dirty_ref, bf16[1024,256]{1,0:T(8,128)(2,1)S(1)} %copy-done, bf16[256,768]{1,0:T(8,128)(2,1)S(1)} %copy-done.1), custom_call_target="tpu_custom_call" | custom-call | tf_op jit(solution)/shard_map/pallas_call | solution.py:399
  38.3 0.6 %collective-permute-start.6 = (f32[256,256]{1,0:T(8,128)S(1)}, f32[256,256]{1,0:T(8,128)S(1)}, u32[]{:S(2)}, u32[]{:S(2)}) collective-permute-start(f32[256,256]{1,0:T(8,128)S(1)} %shard_map.110), channel_id=1, source_target_pairs={{0,32},{32,0},{64,96},{96,64},{1,33},{33,1},{65,97},{97,65},{2,34}... | collective-permute-start | bytes 786440 | tf_op jit(solution)/shard_map/ppermute | solution.py:474
  38.9 0.0 collective-permute-done.7.refs_1_
  38.9 0.1 collective-permute-start.8
  39.0 1.1 %shard_map.109.refs_0_ = f32[256,256]{1,0:T(8,128)S(1)} custom-call(f32[1,384,512]{2,1,0:T(8,128)S(1)} %get-tuple-element.21.x_ref, f32[4,384,512]{2,1,0:T(8,128)S(1)} %kernel_spectra.1.y_ref, f32[4,256,256]{2,1,0:T(8,128)S(1)} %dirty_sums.1.dirty_ref, bf16[1024,256]{1,0:T(8,128)(2,1)S(1)} %copy-done, bf16[256,768]{1,0:T(8,128)(2,1)S(1)} %copy-done.1), custom_call_target="tpu_custom_call" | custom-call | tf_op jit(solution)/shard_map/pallas_call | solution.py:399
  40.1 0.0 collective-permute-done.6.refs_1_
  40.2 7.1 %collective-permute-done.8.refs_2_ = f32[256,256]{1,0:T(8,128)S(1)} collective-permute-done((f32[256,256]{1,0:T(8,128)S(1)}, f32[256,256]{1,0:T(8,128)S(1)}, u32[]{:S(2)}, u32[]{:S(2)}) %collective-permute-start.8) | collective-permute-done | bytes 262176 | tf_op jit(solution)/shard_map/ppermute | solution.py:472
  47.3 0.7 %shard_map.113 = f32[256,256]{1,0:T(8,128)} custom-call(f32[256,256]{1,0:T(8,128)S(1)} %shard_map.109.refs_0_, f32[256,256]{1,0:T(8,128)S(1)} %collective-permute-done.6.refs_1_, f32[256,256]{1,0:T(8,128)S(1)} %collective-permute-done.8.refs_2_), custom_call_target="tpu_custom_call" | custom-call | tf_op jit(solution)/shard_map/pallas_call | solution.py:417
  (1 shorter events, 0.0 us)
Async XLA Ops:
  0.0 30.4 %copy-start.3 = (bf16[384,768]{1,0:T(8,128)(2,1)S(1)}, bf16[384,768]{1,0:T(8,128)(2,1)}, u32[]{:S(2)}) copy-start(bf16[384,768]{1,0:T(8,128)(2,1)} %constant.15.clone.fr_ref) | copy-start | bytes 1769476
  0.0 30.4 %copy-start.2 = (bf16[768,512]{1,0:T(8,128)(2,1)S(1)}, bf16[768,512]{1,0:T(8,128)(2,1)}, u32[]{:S(2)}) copy-start(bf16[768,512]{1,0:T(8,128)(2,1)} %constant.14.clone.fc_ref) | copy-start | bytes 2359300
  1.6 29.9 %copy-start.4 = (bf16[384,288]{1,0:T(8,128)(2,1)S(1)}, bf16[384,288]{1,0:T(8,128)(2,1)}, u32[]{:S(2)}) copy-start(bf16[384,288]{1,0:T(8,128)(2,1)} %constant.17.clone.gr_ref) | copy-start | bytes 663556
  1.6 29.9 %copy-start.5 = (bf16[256,512]{1,0:T(8,128)(2,1)S(1)}, bf16[256,512]{1,0:T(8,128)(2,1)}, u32[]{:S(2)}) copy-start(bf16[256,512]{1,0:T(8,128)(2,1)} %constant.16.clone.gc_ref) | copy-start | bytes 786436
  1.6 29.8 %copy-start.6 = (f32[8,512]{1,0:T(8,128)S(1)}, f32[8,512]{1,0:T(8,128)}, u32[]{:S(2)}) copy-start(f32[8,512]{1,0:T(8,128)} %constant.20.clone.edge_ref) | copy-start | bytes 49156
  1.6 1.9 %collective-permute-start.4 = (f32[7,136,128]{2,1,0:T(8,128)S(1)}, f32[7,136,128]{2,1,0:T(8,128)S(1)}, u32[]{:S(2)}, u32[]{:S(2)}) collective-permute-start(f32[7,136,128]{2,1,0:T(8,128)S(1)} %moments.1.mine_ref), channel_id=1, source_target_pairs={{0,32},{32,0},{64,96},{96,64},{1,33},{33,1},{65,97},{97,65},{2,34}... | collective-permute-start | bytes 1462280 | tf_op jit(solution)/shard_map/ppermute | solution.py:458
  3.6 27.8 %collective-permute-start.5 = (f32[4,136,128]{2,1,0:T(8,128)S(1)}, f32[4,136,128]{2,1,0:T(8,128)S(1)}, u32[]{:S(2)}, u32[]{:S(2)}) collective-permute-start(f32[4,136,128]{2,1,0:T(8,128)S(1)} %get-tuple-element.20), channel_id=1, source_target_pairs={{0,64},{64,0},{32,96},{96,32},{1,65},{65,1},{33,97},{97,33},{2,66}... | collective-permute-start | bytes 835592 | tf_op jit(solution)/shard_map/ppermute | solution.py:460
  6.7 4.7 %collective-permute-start = (f32[128,128]{1,0:T(8,128)S(1)}, f32[128,128]{1,0:T(8,128)S(1)}, u32[]{:S(2)}, u32[]{:S(2)}) collective-permute-start(f32[128,128]{1,0:T(8,128)S(1)} %get-tuple-element.15), channel_id=1, source_target_pairs={{26,27},{27,26},{28,29},{29,28},{30,31},{31,30},{0,1},{1,0},{2,3},... | collective-permute-start | bytes 196616 | tf_op jit(solution)/shard_map/ppermute | solution.py:456
  7.5 8.3 %collective-permute-start.1 = (f32[128,128]{1,0:T(8,128)S(1)}, f32[128,128]{1,0:T(8,128)S(1)}, u32[]{:S(2)}, u32[]{:S(2)}) collective-permute-start(f32[128,128]{1,0:T(8,128)S(1)} %get-tuple-element.16), channel_id=1, source_target_pairs={{27,28},{28,27},{31,0},{0,31},{3,4},{4,3},{7,8},{8,7},{11,12},{12,... | collective-permute-start | bytes 196616 | tf_op jit(solution)/shard_map/ppermute | solution.py:455
  15.8 18.2 %collective-permute-start.2 = (f32[64,384]{1,0:T(8,128)S(1)}, f32[64,384]{1,0:T(8,128)S(1)}, u32[]{:S(2)}, u32[]{:S(2)}) collective-permute-start(f32[64,384]{1,0:T(8,128)S(1)} %get-tuple-element.17), channel_id=1, source_target_pairs={{26,30},{30,26},{27,31},{31,27},{0,4},{4,0},{1,5},{5,1},{2,6},{6,2... | collective-permute-start | bytes 294920 | tf_op jit(solution)/shard_map/ppermute | solution.py:463
  19.3 14.8 %collective-permute-start.3 = (f32[64,384]{1,0:T(8,128)S(1)}, f32[64,384]{1,0:T(8,128)S(1)}, u32[]{:S(2)}, u32[]{:S(2)}) collective-permute-start(f32[64,384]{1,0:T(8,128)S(1)} %get-tuple-element.18), channel_id=1, source_target_pairs={{28,0},{0,28},{29,1},{1,29},{30,2},{2,30},{31,3},{3,31},{4,8},{8,4... | collective-permute-start | bytes 294920 | tf_op jit(solution)/shard_map/ppermute | solution.py:462
  30.4 3.6 %copy-start = (bf16[1024,256]{1,0:T(8,128)(2,1)S(1)}, bf16[1024,256]{1,0:T(8,128)(2,1)}, u32[]{:S(2)}) copy-start(bf16[1024,256]{1,0:T(8,128)(2,1)} %constant.18.clone.dc_ref) | copy-start | bytes 1572868
  30.4 3.6 %copy-start.1 = (bf16[256,768]{1,0:T(8,128)(2,1)S(1)}, bf16[256,768]{1,0:T(8,128)(2,1)}, u32[]{:S(2)}) copy-start(bf16[256,768]{1,0:T(8,128)(2,1)} %constant.19.clone.dr_ref) | copy-start | bytes 1179652
  36.0 2.9 %collective-permute-start.7 = (f32[256,256]{1,0:T(8,128)S(1)}, f32[256,256]{1,0:T(8,128)S(1)}, u32[]{:S(2)}, u32[]{:S(2)}) collective-permute-start(f32[256,256]{1,0:T(8,128)S(1)} %get-tuple-element.22), channel_id=1, source_target_pairs={{0,32},{32,0},{64,96},{96,64},{1,33},{33,1},{65,97},{97,65},{2,34}... | collective-permute-start | bytes 786440 | tf_op jit(solution)/shard_map/ppermute | solution.py:469
  38.3 1.8 %collective-permute-start.6 = (f32[256,256]{1,0:T(8,128)S(1)}, f32[256,256]{1,0:T(8,128)S(1)}, u32[]{:S(2)}, u32[]{:S(2)}) collective-permute-start(f32[256,256]{1,0:T(8,128)S(1)} %shard_map.110), channel_id=1, source_target_pairs={{0,32},{32,0},{64,96},{96,64},{1,33},{33,1},{65,97},{97,65},{2,34}... | collective-permute-start | bytes 786440 | tf_op jit(solution)/shard_map/ppermute | solution.py:474
  38.9 8.3 %collective-permute-start.8 = (f32[256,256]{1,0:T(8,128)S(1)}, f32[256,256]{1,0:T(8,128)S(1)}, u32[]{:S(2)}, u32[]{:S(2)}) collective-permute-start(f32[256,256]{1,0:T(8,128)S(1)} %shard_map.112), channel_id=1, source_target_pairs={{0,64},{64,0},{32,96},{96,32},{1,65},{65,1},{33,97},{97,33},{2,66}... | collective-permute-start | bytes 786440 | tf_op jit(solution)/shard_map/ppermute | solution.py:472

commit v3 on v2

--- a/solution.py
+++ b/solution.py
@@ -25,6 +25,7 @@
 KP = 144
 KW = 136
 MOMENTS = 2 * TERMS - 1
+OFFSET = FGY + FGY // 2
 DIRTY_PARTS = 4
 
 F32 = jnp.float32
@@ -125,9 +126,14 @@
 
 
 def pack_kernel(x_hbm, x_ref, near_ref, far_ref, sem):
-    copy = pltpu.make_async_copy(x_hbm, x_ref, sem)
-    copy.start()
-    copy.wait()
+    copies = []
+    for start in range(0, P_SIZE, 32):
+        part = pl.ds(start, 32)
+        copies.append(pltpu.make_async_copy(x_hbm.at[part], x_ref.at[part], sem.at[start // 32]))
+    for copy in copies:
+        copy.start()
+    for copy in copies:
+        copy.wait()
     odd = lax.axis_index("facet") % 2 == 1
     lane = lax.broadcasted_iota(jnp.int32, (128, 128), 1)
     left, right = x_ref[:, 0:128], x_ref[:, 128:256]
@@ -143,7 +149,7 @@
         out_shape=(shape(P_SIZE, P_SIZE), shape(128, 128), shape(128, 128)),
         in_specs=[HBM],
         out_specs=(VMEM, VMEM, VMEM),
-        scratch_shapes=[pltpu.SemaphoreType.DMA],
+        scratch_shapes=[pltpu.SemaphoreType.DMA((P_SIZE // 32,))],
         compiler_params=grant(2),
         name="pack",
     )(x)
@@ -151,7 +157,10 @@
 
 def side(near, far, half):
     lane = lax.broadcasted_iota(jnp.int32, near.shape, 1)
-    odd = lax.axis_index("facet") % 2 == 1
+    facet = lax.axis_index("facet")
+    odd = facet % 2 == 1
+    column = (facet + OFFSET) % FGY
+    far = jnp.where(jnp.logical_or(column == 0, column == FGY - 1), 0.0, far)
     after, before = jnp.where(odd, far, near), jnp.where(odd, near, far)
     if half == 0:
         return jnp.where(lane < B, after, before)
@@ -368,9 +377,13 @@
 
 def first_kernel(own_ref, near_ref, far_ref, fc_ref, fr_ref, dc_ref, dr_ref, y_ref, dirty_ref,
                  x_ref, out_ref, z_ref):
-    rowodd = lax.axis_index("facet") // FGY % 2 == 1
+    facet = lax.axis_index("facet")
+    odd = facet // FGY % 2 == 1
+    row = (facet + OFFSET) % FACETS // FGY
     near, far = near_ref[...], far_ref[...]
-    halo = jnp.concatenate([jnp.where(rowodd, far, near), jnp.where(rowodd, near, far)], axis=0)
+    below = jnp.where(row == FROWS - 1, 0.0, jnp.where(odd, far, near))
+    above = jnp.where(row == 0, 0.0, jnp.where(odd, near, far))
+    halo = jnp.concatenate([below, above], axis=0)
     cols = times(halo, fc_ref[...])
     high, low = split(cols)
     fr_h, fr_l = fr_ref[:, P_SIZE:NR], fr_ref[:, NR + P_SIZE :]
@@ -421,9 +434,6 @@
         out_specs=VMEM,
         compiler_params=grant(4),
     )(*args)
-
-
-OFFSET = FGY + FGY // 2
 
 
 def facet_at(row, col):
@@ -441,6 +451,10 @@
             if row + 1 < FROWS:
                 there = facet_at(row + 1, col)
                 (near_r if here // FGY % 2 == 0 else far_r).extend([(here, there), (there, here)])
+    for pairs in (near_c, far_c, near_r, far_r):
+        alone = sorted(set(range(FACETS)) - {here for here, _ in pairs})
+        for here, there in zip(alone[0::2], alone[1::2]):
+            pairs.extend([(here, there), (there, here)])
     return near_c, far_c, near_r, far_r
 
 

time: 48.3 us -> 42.6 us (0.88)
  starting transfers between devices: 20.7 us -> 15.2 us
    ppermute x1, starting transfers between devices: 3.88 us -> 1.98 us  [body(): far = lax.ppermute(far, 'facet', far_c)]
    ppermute x1, starting transfers between devices: 3.4 us -> 1.57 us  [body(): near_row = lax.ppermute(near_row, 'facet', near_r)]
    ppermute x1, starting transfers between devices: 9.82 us -> 7.99 us  [body(): far_row = lax.ppermute(far_row, 'facet', far_r)]
    ppermute x1, waiting for transfers between devices: 0.01 us -> 1.54 us  [body(): near = lax.ppermute(near, 'facet', near_c)]
    ppermute x1, waiting for transfers between devices: 4.36 us -> 2.85 us  [body(): far = lax.ppermute(far, 'facet', far_c)]
  transfers between devices with their start and end apart: 9 -> 9, of which waited for: 3 -> 4; matrix products, arithmetic and copies ran while one was open for 0% -> 0% of each run, Pallas kernels for 19% -> 22%
where the time goes in v3:
time: 42.6 us; the launch traced here: 42.4 us
  starting transfers between devices  15.2 us (36%)
  Pallas kernels  13.6 us (32%)
  waiting for transfers between devices  13.3 us (31%)
    ppermute x1, starting transfers between devices, body(): far_row = lax.ppermute(far_row, 'facet', far_r)  7.99 us
    ppermute x1, waiting for transfers between devices, body(): remote = lax.ppermute(remote, 'band', CHIPS)  7.09 us
    pallas_call x3, Pallas kernels, back(): pl.pallas_call(functools.partial(back_kernel, chip, core), in_specs=[VMEM...  3.34 us
    ppermute x1, waiting for transfers between devices, body(): far = lax.ppermute(far, 'facet', far_c)  2.85 us
    pallas_call x1, Pallas kernels, kernel_spectra(): pl.pallas_call(kernels_kernel, grid=(TERMS,), out_shape=shape(TERMS, NR,...  2.56 us
    ppermute x1, starting transfers between devices, body(): got = lax.ppermute(send, 'band', CHIPS)  2 us
    ppermute x1, starting transfers between devices, body(): far = lax.ppermute(far, 'facet', far_c)  1.98 us
    pallas_call x1, Pallas kernels, first(): pl.pallas_call(first_kernel, in_specs=[VMEM] * len(args), out_specs=(VMEM...  1.96 us
  transfers between devices with their start and end apart: 9, of which 4 were waited for; matrix products, arithmetic and copies ran while one was open for 0% of the time, Pallas kernels for 22%

profile of v3, /device:TPU:24, one launch (start us, length us, event | category | flops | bytes accessed | tf_op | source)
XLA Modules:
  0.0 42.4 jit_solution(8807530941301368598)
XLA Ops:
  0.0 0.0 copy-start.3
  0.0 0.0 copy-start.2
  0.0 1.5 %moments.1.mine_ref = f32[7,136,128]{2,1,0:T(8,128)S(1)} custom-call(f32[4]{0:T(128)} %off_hbm.3, f32[4,129,1,129]{3,2,1,0:T(1,128)} %bitcast.3), custom_call_target="tpu_custom_call" | custom-call | tf_op jit(solution)/shard_map/moments/pallas_call | solution.py:255
  1.6 0.0 copy-start.4
  1.6 0.0 copy-start.5
  1.6 0.0 copy-start.6
  1.6 0.1 collective-permute-start.4
  1.7 1.8 %collective-permute-done.4.got_ref = f32[7,136,128]{2,1,0:T(8,128)S(1)} collective-permute-done((f32[7,136,128]{2,1,0:T(8,128)S(1)}, f32[7,136,128]{2,1,0:T(8,128)S(1)}, u32[]{:S(2)}, u32[]{:S(2)}) %collective-permute-start.4) | collective-permute-done | bytes 487456 | tf_op jit(solution)/shard_map/ppermute | solution.py:472
  3.5 0.1 combine.1
  3.6 2.0 %collective-permute-start.5 = (f32[4,136,128]{2,1,0:T(8,128)S(1)}, f32[4,136,128]{2,1,0:T(8,128)S(1)}, u32[]{:S(2)}, u32[]{:S(2)}) collective-permute-start(f32[4,136,128]{2,1,0:T(8,128)S(1)} %get-tuple-element.20), channel_id=1, source_target_pairs={{0,64},{64,0},{32,96},{96,32},{1,65},{65,1},{33,97},{97,33},{2,66}... | collective-permute-start | bytes 835592 | tf_op jit(solution)/shard_map/ppermute | solution.py:474
  5.6 1.0 %pack.1 = (f32[256,256]{1,0:T(8,128)S(1)}, f32[128,128]{1,0:T(8,128)S(1)}, f32[128,128]{1,0:T(8,128)S(1)}) custom-call(f32[256,256]{1,0:T(8,128)} %bitcast.4), custom_call_target="tpu_custom_call" | custom-call | tf_op jit(solution)/shard_map/pack/pallas_call | solution.py:147
  6.6 0.8 %collective-permute-start = (f32[128,128]{1,0:T(8,128)S(1)}, f32[128,128]{1,0:T(8,128)S(1)}, u32[]{:S(2)}, u32[]{:S(2)}) collective-permute-start(f32[128,128]{1,0:T(8,128)S(1)} %get-tuple-element.15), channel_id=1, source_target_pairs={{26,27},{27,26},{28,29},{29,28},{30,31},{31,30},{0,1},{1,0},{2,3},... | collective-permute-start | bytes 196616 | tf_op jit(solution)/shard_map/ppermute | solution.py:470
  7.5 2.0 %collective-permute-start.1 = (f32[128,128]{1,0:T(8,128)S(1)}, f32[128,128]{1,0:T(8,128)S(1)}, u32[]{:S(2)}, u32[]{:S(2)}) collective-permute-start(f32[128,128]{1,0:T(8,128)S(1)} %get-tuple-element.16), channel_id=1, source_target_pairs={{27,28},{28,27},{31,0},{0,31},{3,4},{4,3},{7,8},{8,7},{11,12},{12,... | collective-permute-start | bytes 196616 | tf_op jit(solution)/shard_map/ppermute | solution.py:469
  9.5 1.5 %collective-permute-done.near_ref = f32[128,128]{1,0:T(8,128)S(1)} collective-permute-done((f32[128,128]{1,0:T(8,128)S(1)}, f32[128,128]{1,0:T(8,128)S(1)}, u32[]{:S(2)}, u32[]{:S(2)}) %collective-permute-start) | collective-permute-done | bytes 65568 | tf_op jit(solution)/shard_map/ppermute | solution.py:470
  11.0 2.9 %collective-permute-done.1.far_ref = f32[128,128]{1,0:T(8,128)S(1)} collective-permute-done((f32[128,128]{1,0:T(8,128)S(1)}, f32[128,128]{1,0:T(8,128)S(1)}, u32[]{:S(2)}, u32[]{:S(2)}) %collective-permute-start.1) | collective-permute-done | bytes 65568 | tf_op jit(solution)/shard_map/ppermute | solution.py:469
  13.8 0.1 edges.1
  13.9 1.6 %collective-permute-start.2 = (f32[64,384]{1,0:T(8,128)S(1)}, f32[64,384]{1,0:T(8,128)S(1)}, u32[]{:S(2)}, u32[]{:S(2)}) collective-permute-start(f32[64,384]{1,0:T(8,128)S(1)} %get-tuple-element.17), channel_id=1, source_target_pairs={{26,30},{30,26},{27,31},{31,27},{0,4},{4,0},{1,5},{5,1},{2,6},{6,2... | collective-permute-start | bytes 294920 | tf_op jit(solution)/shard_map/ppermute | solution.py:477
  15.5 8.0 %collective-permute-start.3 = (f32[64,384]{1,0:T(8,128)S(1)}, f32[64,384]{1,0:T(8,128)S(1)}, u32[]{:S(2)}, u32[]{:S(2)}) collective-permute-start(f32[64,384]{1,0:T(8,128)S(1)} %get-tuple-element.18), channel_id=1, source_target_pairs={{28,0},{0,28},{29,1},{1,29},{30,2},{2,30},{31,3},{3,31},{4,8},{8,4... | collective-permute-start | bytes 294920 | tf_op jit(solution)/shard_map/ppermute | solution.py:476
  23.5 1.3 %dirty_sums.1.dirty_ref = f32[4,256,256]{2,1,0:T(8,128)S(1)} custom-call(f32[4]{0:T(128)} %off_hbm.3, f32[4,1,256,256]{3,2,1,0:T(8,128)} %dirty_hbm.1), custom_call_target="tpu_custom_call" | custom-call | tf_op jit(solution)/shard_map/dirty_sums/pallas_call | solution.py:343
  24.8 0.0 copy-done.3
  24.8 0.0 copy-done.2
  24.8 0.0 copy-start
  24.8 0.0 copy-start.1
  24.8 0.9 %own_rows.1.own_ref = f32[384,512]{1,0:T(8,128)S(1)} custom-call(f32[256,256]{1,0:T(8,128)S(1)} %get-tuple-element.14.x_ref, f32[128,128]{1,0:T(8,128)S(1)} %collective-permute-done.near_ref, f32[128,128]{1,0:T(8,128)S(1)} %collective-permute-done.1.far_ref, bf16[768,512]{1,0:T(8,128)(2,1)S(1)} %copy-done.2, bf16[384,768]{1,0:T(8,128)(2,1)S(1)} %copy-done.3), custom_call_target="tpu_custom_call" | custom-call | tf_op jit(solution)/shard_map/own_rows/pallas_call | solution.py:203
  25.8 0.0 collective-permute-done.5.got_ref
  25.8 0.0 copy-done.4
  25.8 0.0 copy-done.5
  25.8 0.0 copy-done.6
  25.8 2.6 %kernel_spectra.1.y_ref = f32[4,384,512]{2,1,0:T(8,128)S(1)} custom-call(f32[4,136,128]{2,1,0:T(8,128)S(1)} %get-tuple-element.19.mine_ref, f32[4,136,128]{2,1,0:T(8,128)S(1)} %collective-permute-done.5.got_ref, bf16[256,512]{1,0:T(8,128)(2,1)S(1)} %copy-done.5, bf16[384,288]{1,0:T(8,128)(2,1)S(1)} %copy-done.4, f32[8,512]{1,0:T(8,128)S(1)} %copy-done.6), custom_call_target="tpu_custom_call" | custom-call | tf_op jit(solution)/shard_map/kernel_spectra/pallas_call | solution.py:306
  28.4 0.0 collective-permute-done.2.near_ref
  28.4 0.0 collective-permute-done.3.far_ref
  28.4 0.0 copy-done
  28.4 0.0 copy-done.1
  28.4 2.0 %first.1 = (f32[1,384,512]{2,1,0:T(8,128)S(1)}, f32[256,256]{1,0:T(8,128)S(1)}) custom-call(f32[384,512]{1,0:T(8,128)S(1)} %own_rows.1.own_ref, f32[64,384]{1,0:T(8,128)S(1)} %collective-permute-done.2.near_ref, f32[64,384]{1,0:T(8,128)S(1)} %collective-permute-done.3.far_ref, bf16[768,512]{1,0:T(8,128)(2,1)S(1)} %copy-done.2, ...), custom_call_target="tpu_custom_call" | custom-call | tf_op jit(solution)/shard_map/first/pallas_call | solution.py:396
  30.4 0.1 collective-permute-start.7
  30.5 1.1 %shard_map.111.refs_0_ = f32[256,256]{1,0:T(8,128)S(1)} custom-call(f32[1,384,512]{2,1,0:T(8,128)S(1)} %get-tuple-element.21.x_ref, f32[4,384,512]{2,1,0:T(8,128)S(1)} %kernel_spectra.1.y_ref, f32[4,256,256]{2,1,0:T(8,128)S(1)} %dirty_sums.1.dirty_ref, bf16[1024,256]{1,0:T(8,128)(2,1)S(1)} %copy-done, bf16[256,768]{1,0:T(8,128)(2,1)S(1)} %copy-done.1), custom_call_target="tpu_custom_call" | custom-call | tf_op jit(solution)/shard_map/pallas_call | solution.py:412
  31.6 1.1 %shard_map.110 = f32[256,256]{1,0:T(8,128)S(1)} custom-call(f32[1,384,512]{2,1,0:T(8,128)S(1)} %get-tuple-element.21.x_ref, f32[4,384,512]{2,1,0:T(8,128)S(1)} %kernel_spectra.1.y_ref, f32[4,256,256]{2,1,0:T(8,128)S(1)} %dirty_sums.1.dirty_ref, bf16[1024,256]{1,0:T(8,128)(2,1)S(1)} %copy-done, bf16[256,768]{1,0:T(8,128)(2,1)S(1)} %copy-done.1), custom_call_target="tpu_custom_call" | custom-call | tf_op jit(solution)/shard_map/pallas_call | solution.py:412
  32.7 0.6 %collective-permute-start.6 = (f32[256,256]{1,0:T(8,128)S(1)}, f32[256,256]{1,0:T(8,128)S(1)}, u32[]{:S(2)}, u32[]{:S(2)}) collective-permute-start(f32[256,256]{1,0:T(8,128)S(1)} %shard_map.110), channel_id=1, source_target_pairs={{0,32},{32,0},{64,96},{96,64},{1,33},{33,1},{65,97},{97,65},{2,34}... | collective-permute-start | bytes 786440 | tf_op jit(solution)/shard_map/ppermute | solution.py:488
  33.3 0.0 collective-permute-done.7.refs_1_
  33.4 0.1 collective-permute-start.8
  33.5 1.1 %shard_map.109.refs_0_ = f32[256,256]{1,0:T(8,128)S(1)} custom-call(f32[1,384,512]{2,1,0:T(8,128)S(1)} %get-tuple-element.21.x_ref, f32[4,384,512]{2,1,0:T(8,128)S(1)} %kernel_spectra.1.y_ref, f32[4,256,256]{2,1,0:T(8,128)S(1)} %dirty_sums.1.dirty_ref, bf16[1024,256]{1,0:T(8,128)(2,1)S(1)} %copy-done, bf16[256,768]{1,0:T(8,128)(2,1)S(1)} %copy-done.1), custom_call_target="tpu_custom_call" | custom-call | tf_op jit(solution)/shard_map/pallas_call | solution.py:412
  34.6 0.0 collective-permute-done.6.refs_1_
  34.6 7.1 %collective-permute-done.8.refs_2_ = f32[256,256]{1,0:T(8,128)S(1)} collective-permute-done((f32[256,256]{1,0:T(8,128)S(1)}, f32[256,256]{1,0:T(8,128)S(1)}, u32[]{:S(2)}, u32[]{:S(2)}) %collective-permute-start.8) | collective-permute-done | bytes 262176 | tf_op jit(solution)/shard_map/ppermute | solution.py:486
  41.7 0.7 %shard_map.113 = f32[256,256]{1,0:T(8,128)} custom-call(f32[256,256]{1,0:T(8,128)S(1)} %shard_map.109.refs_0_, f32[256,256]{1,0:T(8,128)S(1)} %collective-permute-done.6.refs_1_, f32[256,256]{1,0:T(8,128)S(1)} %collective-permute-done.8.refs_2_), custom_call_target="tpu_custom_call" | custom-call | tf_op jit(solution)/shard_map/pallas_call | solution.py:430
  (1 shorter events, 0.0 us)
Async XLA Ops:
  0.0 24.8 %copy-start.3 = (bf16[384,768]{1,0:T(8,128)(2,1)S(1)}, bf16[384,768]{1,0:T(8,128)(2,1)}, u32[]{:S(2)}) copy-start(bf16[384,768]{1,0:T(8,128)(2,1)} %constant.15.clone.fr_ref) | copy-start | bytes 1769476
  0.0 24.8 %copy-start.2 = (bf16[768,512]{1,0:T(8,128)(2,1)S(1)}, bf16[768,512]{1,0:T(8,128)(2,1)}, u32[]{:S(2)}) copy-start(bf16[768,512]{1,0:T(8,128)(2,1)} %constant.14.clone.fc_ref) | copy-start | bytes 2359300
  1.6 24.2 %copy-start.4 = (bf16[384,288]{1,0:T(8,128)(2,1)S(1)}, bf16[384,288]{1,0:T(8,128)(2,1)}, u32[]{:S(2)}) copy-start(bf16[384,288]{1,0:T(8,128)(2,1)} %constant.17.clone.gr_ref) | copy-start | bytes 663556
  1.6 24.2 %copy-start.5 = (bf16[256,512]{1,0:T(8,128)(2,1)S(1)}, bf16[256,512]{1,0:T(8,128)(2,1)}, u32[]{:S(2)}) copy-start(bf16[256,512]{1,0:T(8,128)(2,1)} %constant.16.clone.gc_ref) | copy-start | bytes 786436
  1.6 24.2 %copy-start.6 = (f32[8,512]{1,0:T(8,128)S(1)}, f32[8,512]{1,0:T(8,128)}, u32[]{:S(2)}) copy-start(f32[8,512]{1,0:T(8,128)} %constant.20.clone.edge_ref) | copy-start | bytes 49156
  1.6 1.9 %collective-permute-start.4 = (f32[7,136,128]{2,1,0:T(8,128)S(1)}, f32[7,136,128]{2,1,0:T(8,128)S(1)}, u32[]{:S(2)}, u32[]{:S(2)}) collective-permute-start(f32[7,136,128]{2,1,0:T(8,128)S(1)} %moments.1.mine_ref), channel_id=1, source_target_pairs={{0,32},{32,0},{64,96},{96,64},{1,33},{33,1},{65,97},{97,65},{2,34}... | collective-permute-start | bytes 1462280 | tf_op jit(solution)/shard_map/ppermute | solution.py:472
  3.6 22.2 %collective-permute-start.5 = (f32[4,136,128]{2,1,0:T(8,128)S(1)}, f32[4,136,128]{2,1,0:T(8,128)S(1)}, u32[]{:S(2)}, u32[]{:S(2)}) collective-permute-start(f32[4,136,128]{2,1,0:T(8,128)S(1)} %get-tuple-element.20), channel_id=1, source_target_pairs={{0,64},{64,0},{32,96},{96,32},{1,65},{65,1},{33,97},{97,33},{2,66}... | collective-permute-start | bytes 835592 | tf_op jit(solution)/shard_map/ppermute | solution.py:474
  6.6 4.3 %collective-permute-start = (f32[128,128]{1,0:T(8,128)S(1)}, f32[128,128]{1,0:T(8,128)S(1)}, u32[]{:S(2)}, u32[]{:S(2)}) collective-permute-start(f32[128,128]{1,0:T(8,128)S(1)} %get-tuple-element.15), channel_id=1, source_target_pairs={{26,27},{27,26},{28,29},{29,28},{30,31},{31,30},{0,1},{1,0},{2,3},... | collective-permute-start | bytes 196616 | tf_op jit(solution)/shard_map/ppermute | solution.py:470
  7.5 6.4 %collective-permute-start.1 = (f32[128,128]{1,0:T(8,128)S(1)}, f32[128,128]{1,0:T(8,128)S(1)}, u32[]{:S(2)}, u32[]{:S(2)}) collective-permute-start(f32[128,128]{1,0:T(8,128)S(1)} %get-tuple-element.16), channel_id=1, source_target_pairs={{27,28},{28,27},{31,0},{0,31},{3,4},{4,3},{7,8},{8,7},{11,12},{12,... | collective-permute-start | bytes 196616 | tf_op jit(solution)/shard_map/ppermute | solution.py:469
  13.9 14.5 %collective-permute-start.2 = (f32[64,384]{1,0:T(8,128)S(1)}, f32[64,384]{1,0:T(8,128)S(1)}, u32[]{:S(2)}, u32[]{:S(2)}) collective-permute-start(f32[64,384]{1,0:T(8,128)S(1)} %get-tuple-element.17), channel_id=1, source_target_pairs={{26,30},{30,26},{27,31},{31,27},{0,4},{4,0},{1,5},{5,1},{2,6},{6,2... | collective-permute-start | bytes 294920 | tf_op jit(solution)/shard_map/ppermute | solution.py:477
  15.5 12.9 %collective-permute-start.3 = (f32[64,384]{1,0:T(8,128)S(1)}, f32[64,384]{1,0:T(8,128)S(1)}, u32[]{:S(2)}, u32[]{:S(2)}) collective-permute-start(f32[64,384]{1,0:T(8,128)S(1)} %get-tuple-element.18), channel_id=1, source_target_pairs={{28,0},{0,28},{29,1},{1,29},{30,2},{2,30},{31,3},{3,31},{4,8},{8,4... | collective-permute-start | bytes 294920 | tf_op jit(solution)/shard_map/ppermute | solution.py:476
  24.8 3.6 %copy-start = (bf16[1024,256]{1,0:T(8,128)(2,1)S(1)}, bf16[1024,256]{1,0:T(8,128)(2,1)}, u32[]{:S(2)}) copy-start(bf16[1024,256]{1,0:T(8,128)(2,1)} %constant.18.clone.dc_ref) | copy-start | bytes 1572868
  24.8 3.6 %copy-start.1 = (bf16[256,768]{1,0:T(8,128)(2,1)S(1)}, bf16[256,768]{1,0:T(8,128)(2,1)}, u32[]{:S(2)}) copy-start(bf16[256,768]{1,0:T(8,128)(2,1)} %constant.19.clone.dr_ref) | copy-start | bytes 1179652
  30.4 2.9 %collective-permute-start.7 = (f32[256,256]{1,0:T(8,128)S(1)}, f32[256,256]{1,0:T(8,128)S(1)}, u32[]{:S(2)}, u32[]{:S(2)}) collective-permute-start(f32[256,256]{1,0:T(8,128)S(1)} %get-tuple-element.22), channel_id=1, source_target_pairs={{0,32},{32,0},{64,96},{96,64},{1,33},{33,1},{65,97},{97,65},{2,34}... | collective-permute-start | bytes 786440 | tf_op jit(solution)/shard_map/ppermute | solution.py:483
  32.7 1.8 %collective-permute-start.6 = (f32[256,256]{1,0:T(8,128)S(1)}, f32[256,256]{1,0:T(8,128)S(1)}, u32[]{:S(2)}, u32[]{:S(2)}) collective-permute-start(f32[256,256]{1,0:T(8,128)S(1)} %shard_map.110), channel_id=1, source_target_pairs={{0,32},{32,0},{64,96},{96,64},{1,33},{33,1},{65,97},{97,65},{2,34}... | collective-permute-start | bytes 786440 | tf_op jit(solution)/shard_map/ppermute | solution.py:488
  33.4 8.3 %collective-permute-start.8 = (f32[256,256]{1,0:T(8,128)S(1)}, f32[256,256]{1,0:T(8,128)S(1)}, u32[]{:S(2)}, u32[]{:S(2)}) collective-permute-start(f32[256,256]{1,0:T(8,128)S(1)} %shard_map.112), channel_id=1, source_target_pairs={{0,64},{64,0},{32,96},{96,32},{1,65},{65,1},{33,97},{97,33},{2,66}... | collective-permute-start | bytes 786440 | tf_op jit(solution)/shard_map/ppermute | solution.py:486

commit v4 on v3

--- a/solution.py
+++ b/solution.py
@@ -125,15 +125,14 @@
     return jax.ShapeDtypeStruct(dims, dtype)
 
 
-def pack_kernel(x_hbm, x_ref, near_ref, far_ref, sem):
-    copies = []
-    for start in range(0, P_SIZE, 32):
-        part = pl.ds(start, 32)
-        copies.append(pltpu.make_async_copy(x_hbm.at[part], x_ref.at[part], sem.at[start // 32]))
+def prepare_kernel(x_hbm, off_hbm, psf_hbm, x_ref, near_ref, far_ref, out_ref, off_ref, psf_ref, sems):
+    image = pltpu.make_async_copy(x_hbm, x_ref, sems.at[0])
+    copies = [pltpu.make_async_copy(off_hbm, off_ref, sems.at[1])]
+    copies += [pltpu.make_async_copy(psf_hbm.at[b, :, 0, :], psf_ref.at[b], sems.at[2 + b]) for b in range(4)]
+    image.start()
     for copy in copies:
         copy.start()
-    for copy in copies:
-        copy.wait()
+    image.wait()
     odd = lax.axis_index("facet") % 2 == 1
     lane = lax.broadcasted_iota(jnp.int32, (128, 128), 1)
     left, right = x_ref[:, 0:128], x_ref[:, 128:256]
@@ -141,80 +140,6 @@
     right = jnp.where(lane < B, pltpu.roll(right[128:256], B, 1), right[0:128])
     near_ref[...] = jnp.where(odd, left, right)
     far_ref[...] = jnp.where(odd, right, left)
-
-
-def pack(x):
-    return pl.pallas_call(
-        pack_kernel,
-        out_shape=(shape(P_SIZE, P_SIZE), shape(128, 128), shape(128, 128)),
-        in_specs=[HBM],
-        out_specs=(VMEM, VMEM, VMEM),
-        scratch_shapes=[pltpu.SemaphoreType.DMA((P_SIZE // 32,))],
-        compiler_params=grant(2),
-        name="pack",
-    )(x)
-
-
-def side(near, far, half):
-    lane = lax.broadcasted_iota(jnp.int32, near.shape, 1)
-    facet = lax.axis_index("facet")
-    odd = facet % 2 == 1
-    column = (facet + OFFSET) % FGY
-    far = jnp.where(jnp.logical_or(column == 0, column == FGY - 1), 0.0, far)
-    after, before = jnp.where(odd, far, near), jnp.where(odd, near, far)
-    if half == 0:
-        return jnp.where(lane < B, after, before)
-    return jnp.where(lane < B, pltpu.roll(after, B, 1), pltpu.roll(before, B, 1))
-
-
-def edges_kernel(x_ref, near_ref, far_ref, near_out, far_out):
-    odd = lax.axis_index("facet") // FGY % 2 == 1
-    top = side(near_ref[0:B, :], far_ref[0:B, :], 0)
-    bottom = side(near_ref[B:, :], far_ref[B:, :], 1)
-    for lanes, above, below in (
-        (slice(0, 256), x_ref[0:B, :], x_ref[256 - B : 256, :]),
-        (slice(256, 384), top, bottom),
-    ):
-        near_out[:, lanes] = jnp.where(odd, above, below)
-        far_out[:, lanes] = jnp.where(odd, below, above)
-
-
-def edges(x, near, far):
-    return pl.pallas_call(
-        edges_kernel,
-        out_shape=(shape(B, SPAN), shape(B, SPAN)),
-        in_specs=[VMEM] * 3,
-        out_specs=(VMEM, VMEM),
-        compiler_params=grant(2),
-        name="edges",
-    )(x, near, far)
-
-
-def own_kernel(x_ref, near_ref, far_ref, fc_ref, fr_ref, out_ref):
-    near, far = near_ref[...], far_ref[...]
-    borders = jnp.concatenate([side(near, far, 0), side(near, far, 1)], axis=0)
-    cols = times(jnp.concatenate([x_ref[...], borders], axis=1), fc_ref[...])
-    high, low = split(cols)
-    fr_h, fr_l = fr_ref[:, 0:P_SIZE], fr_ref[:, NR : NR + P_SIZE]
-    out_ref[...] = mix(fr_h, fr_l, high, low)
-
-
-def own_rows(*args):
-    return pl.pallas_call(
-        own_kernel,
-        out_shape=shape(NR, NC),
-        in_specs=[VMEM] * 5,
-        out_specs=VMEM,
-        compiler_params=grant(8),
-        name="own_rows",
-    )(*args)
-
-
-def moments_kernel(off_hbm, psf_hbm, out_ref, off_ref, psf_ref, sems):
-    copies = [pltpu.make_async_copy(psf_hbm.at[b, :, 0, :], psf_ref.at[b], sems.at[b]) for b in range(4)]
-    copies.append(pltpu.make_async_copy(off_hbm, off_ref, sems.at[4]))
-    for copy in copies:
-        copy.start()
     for copy in copies:
         copy.wait()
     weights = []
@@ -251,20 +176,81 @@
         out_ref[s, 128:KW, :] = jnp.concatenate(rows + [rest], axis=0)
 
 
-def moments(off, psf):
-    return pl.pallas_call(
-        moments_kernel,
-        out_shape=shape(MOMENTS, KW, 128),
-        in_specs=[HBM, HBM],
-        out_specs=VMEM,
+def prepare(x, off, psf):
+    return pl.pallas_call(
+        prepare_kernel,
+        out_shape=(shape(P_SIZE, P_SIZE), shape(128, 128), shape(128, 128), shape(MOMENTS, KW, 128)),
+        in_specs=[HBM, HBM, HBM],
+        out_specs=(VMEM,) * 4,
         scratch_shapes=[
             pltpu.SMEM((4,), F32),
             pltpu.VMEM((4, K, K), F32),
-            pltpu.SemaphoreType.DMA((5,)),
+            pltpu.SemaphoreType.DMA((6,)),
         ],
         compiler_params=grant(4),
-        name="moments",
-    )(in_hbm(off), in_hbm(jnp.transpose(psf, (0, 2, 1, 3))))
+        name="prepare",
+    )(in_hbm(x), in_hbm(off), in_hbm(jnp.transpose(psf, (0, 2, 1, 3))))
+
+
+def side(near, far, half):
+    lane = lax.broadcasted_iota(jnp.int32, near.shape, 1)
+    facet = lax.axis_index("facet")
+    odd = facet % 2 == 1
+    column = (facet + OFFSET) % FGY
+    far = jnp.where(jnp.logical_or(column == 0, column == FGY - 1), 0.0, far)
+    after, before = jnp.where(odd, far, near), jnp.where(odd, near, far)
+    if half == 0:
+        return jnp.where(lane < B, after, before)
+    return jnp.where(lane < B, pltpu.roll(after, B, 1), pltpu.roll(before, B, 1))
+
+
+def edges_kernel(x_ref, near_ref, far_ref, near_out, far_out):
+    odd = lax.axis_index("facet") // FGY % 2 == 1
+    top = side(near_ref[0:B, :], far_ref[0:B, :], 0)
+    bottom = side(near_ref[B:, :], far_ref[B:, :], 1)
+    for lanes, above, below in (
+        (slice(0, 256), x_ref[0:B, :], x_ref[256 - B : 256, :]),
+        (slice(256, 384), top, bottom),
+    ):
+        near_out[:, lanes] = jnp.where(odd, above, below)
+        far_out[:, lanes] = jnp.where(odd, below, above)
+
+
+def edges(x, near, far):
+    return pl.pallas_call(
+        edges_kernel,
+        out_shape=(shape(B, SPAN), shape(B, SPAN)),
+        in_specs=[VMEM] * 3,
+        out_specs=(VMEM, VMEM),
+        compiler_params=grant(2),
+        name="edges",
+    )(x, near, far)
+
+
+def own_kernel(x_ref, near_ref, far_ref, fc_ref, fr_ref, out_ref):
+    near, far = near_ref[...], far_ref[...]
+    borders = jnp.concatenate([side(near, far, 0), side(near, far, 1)], axis=0)
+    cols = times(jnp.concatenate([x_ref[...], borders], axis=1), fc_ref[...])
+    high, low = split(cols)
+    fr_h, fr_l = fr_ref[:, 0:P_SIZE], fr_ref[:, NR : NR + P_SIZE]
+    x = mix(fr_h, fr_l, high, low)
+    diagonal(out_ref, x[0:HR, 0:HC], x[0:HR, HC:NC], x[HR:NR, 0:HC], x[HR:NR, HC:NC])
+
+
+def own_rows(*args):
+    return pl.pallas_call(
+        own_kernel,
+        out_shape=shape(1, NR, NC),
+        in_specs=[VMEM] * 5,
+        out_specs=VMEM,
+        compiler_params=grant(8),
+        name="own_rows",
+    )(*args)
+
+
+def target(chip, core):
+    band = lax.axis_index("band")
+    return (band // 2 + chip) % 2 * 2 + (band + core) % 2
 
 
 def terms():
@@ -272,19 +258,25 @@
     return band, (band + 2) % 4
 
 
-def combine_kernel(mine_ref, got_ref, keep_ref, send_ref):
+def combine_kernel(mine_ref, got_ref, leaves_ref, stays_ref, send_leaves_ref, send_stays_ref):
     own, other = terms()
-    for j in range(TERMS):
-        keep_ref[j] = mine_ref[own + j] + got_ref[own + j]
-        send_ref[j] = mine_ref[other + j] + got_ref[other + j]
+    for core in range(2):
+        for term, chip, ref in (
+            (own, 1, leaves_ref),
+            (own, 0, stays_ref),
+            (other, 0, send_leaves_ref),
+            (other, 1, send_stays_ref),
+        ):
+            s = term + target(chip, core)
+            ref[core] = mine_ref[s] + got_ref[s]
 
 
 def combine(mine, got):
     return pl.pallas_call(
         combine_kernel,
-        out_shape=(shape(TERMS, KW, 128), shape(TERMS, KW, 128)),
+        out_shape=(shape(2, KW, 128),) * 4,
         in_specs=[VMEM, VMEM],
-        out_specs=(VMEM, VMEM),
+        out_specs=(VMEM,) * 4,
         compiler_params=grant(4),
         name="combine",
     )(mine, got)
@@ -305,8 +297,8 @@
 def kernel_spectra(*args):
     return pl.pallas_call(
         kernels_kernel,
-        grid=(TERMS,),
-        out_shape=shape(TERMS, NR, NC),
+        grid=(2,),
+        out_shape=shape(2, NR, NC),
         in_specs=[VMEM] * 5,
         out_specs=pl.BlockSpec((1, NR, NC), lambda j: (j, 0, 0)),
         compiler_params=grant(12),
@@ -355,28 +347,32 @@
     )(in_hbm(off), in_hbm(dirty))
 
 
-def target(chip, core):
-    band = lax.axis_index("band")
-    return (band // 2 + chip) % 2 * 2 + (band + core) % 2
-
-
-def product_back(t, x_ref, y_ref, dirty_ref, dc_ref, dr_ref, z_ref):
+ALL = ((0, P_SIZE),)
+MIDDLE = ((B, P_SIZE - B),)
+OUTER = ((0, B), (P_SIZE - B, P_SIZE))
+
+
+def product_back(rows, chip, core, x_ref, y_ref, dirty_ref, dc_ref, dr_ref, out_ref, z_ref):
     a, b = x_ref[0, 0:HR, 0:HC], x_ref[0, HR:NR, 0:HC]
-    c, d = y_ref[t, 0:HR, 0:HC], y_ref[t, HR:NR, 0:HC]
+    c, d = y_ref[core, 0:HR, 0:HC], y_ref[core, HR:NR, 0:HC]
     rp, ip = a * c - b * d, a * d + b * c
     a, b = x_ref[0, 0:HR, HC:NC], x_ref[0, HR:NR, HC:NC]
-    c, d = y_ref[t, 0:HR, HC:NC], y_ref[t, HR:NR, HC:NC]
+    c, d = y_ref[core, 0:HR, HC:NC], y_ref[core, HR:NR, HC:NC]
     rm, im = a * c - b * d, a * d + b * c
     z_ref[0:HR, 0:HC] = rp + rm
     z_ref[0:HR, HC:NC] = ip - im
     z_ref[HR:NR, 0:HC] = ip + im
     z_ref[HR:NR, HC:NC] = rm - rp
     cols = times(z_ref[...], dc_ref[...])
-    return dirty_ref[t] - under(dr_ref[...], cols)
-
-
-def first_kernel(own_ref, near_ref, far_ref, fc_ref, fr_ref, dc_ref, dr_ref, y_ref, dirty_ref,
-                 x_ref, out_ref, z_ref):
+    smeared = under(jnp.concatenate([dr_ref[start:stop] for start, stop in rows], axis=0), cols)
+    term, at = target(chip, core), 0
+    for start, stop in rows:
+        size = stop - start
+        out_ref[at : at + size, :] = dirty_ref[term, start:stop, :] - smeared[at : at + size, :]
+        at += size
+
+
+def first_kernel(own_ref, near_ref, far_ref, fc_ref, fr_ref, y_ref, dirty_ref, dc_ref, dr_ref, x_ref, out_ref, z_ref):
     facet = lax.axis_index("facet")
     odd = facet // FGY % 2 == 1
     row = (facet + OFFSET) % FACETS // FGY
@@ -387,9 +383,10 @@
     cols = times(halo, fc_ref[...])
     high, low = split(cols)
     fr_h, fr_l = fr_ref[:, P_SIZE:NR], fr_ref[:, NR + P_SIZE :]
-    x = own_ref[...] + mix(fr_h, fr_l, high, low)
+    x = mix(fr_h, fr_l, high, low)
     diagonal(x_ref, x[0:HR, 0:HC], x[0:HR, HC:NC], x[HR:NR, 0:HC], x[HR:NR, HC:NC])
-    out_ref[...] = product_back(target(1, 1), x_ref, y_ref, dirty_ref, dc_ref, dr_ref, z_ref)
+    x_ref[...] = x_ref[...] + own_ref[...]
+    product_back(OUTER, 1, 1, x_ref, y_ref, dirty_ref, dc_ref, dr_ref, out_ref, z_ref)
 
 
 def first(*args):
@@ -398,41 +395,55 @@
         in_specs=[VMEM] * len(args),
         out_specs=(VMEM, VMEM),
         scratch_shapes=[pltpu.VMEM((NR, NC), F32)],
-        out_shape=(shape(1, NR, NC), shape(P_SIZE, P_SIZE)),
+        out_shape=(shape(1, NR, NC), shape(2 * B, P_SIZE)),
         compiler_params=grant(12),
         name="first",
     )(*args)
 
 
-def back_kernel(chip, core, x_ref, y_ref, dirty_ref, dc_ref, dr_ref, out_ref, z_ref):
-    out_ref[...] = product_back(target(chip, core), x_ref, y_ref, dirty_ref, dc_ref, dr_ref, z_ref)
-
-
-def back(chip, core, *args):
-    return pl.pallas_call(
-        functools.partial(back_kernel, chip, core),
+def back(rows, chip, core, *args):
+    return pl.pallas_call(
+        functools.partial(product_back, rows, chip, core),
         in_specs=[VMEM] * len(args),
         out_specs=VMEM,
         scratch_shapes=[pltpu.VMEM((NR, NC), F32)],
-        out_shape=shape(P_SIZE, P_SIZE),
+        out_shape=shape(sum(stop - start for start, stop in rows), P_SIZE),
         compiler_params=grant(12),
     )(*args)
 
 
-def total_kernel(*refs):
-    value = refs[0][...]
-    for ref in refs[1:-1]:
-        value = value + ref[...]
-    refs[-1][...] = value
-
-
-def total(*args):
-    return pl.pallas_call(
-        total_kernel,
+def add_kernel(a_ref, b_ref, out_ref):
+    out_ref[...] = a_ref[...] + b_ref[...]
+
+
+def add(a, b):
+    return pl.pallas_call(
+        add_kernel,
+        out_shape=shape(*a.shape),
+        in_specs=[VMEM, VMEM],
+        out_specs=VMEM,
+        compiler_params=grant(2),
+        name="add",
+    )(a, b)
+
+
+def last_kernel(a_ref, b_ref, middle_ref, outer_ref, out_ref):
+    for ref, rows in ((middle_ref, MIDDLE), (outer_ref, OUTER)):
+        at = 0
+        for start, stop in rows:
+            size = stop - start
+            out_ref[start:stop] = (a_ref[start:stop] + b_ref[start:stop]) + ref[at : at + size]
+            at += size
+
+
+def last(*args):
+    return pl.pallas_call(
+        last_kernel,
         out_shape=shape(P_SIZE, P_SIZE),
-        in_specs=[VMEM] * len(args),
+        in_specs=[VMEM] * 4,
         out_specs=VMEM,
-        compiler_params=grant(4),
+        compiler_params=grant(2),
+        name="last",
     )(*args)
 
 
@@ -465,29 +476,36 @@
 def body(coeffs, dirty, psf, band_offset):
     table = {k: jnp.asarray(v) for k, v in tables().items()}
     near_c, far_c, near_r, far_r = exchanges()
-    x, near, far = pack(in_hbm(coeffs[0, 0]))
+    x, near, far, mine = prepare(coeffs[0, 0], band_offset, psf)
+    got = lax.ppermute(mine, "band", CORES)
     far = lax.ppermute(far, "facet", far_c)
     near = lax.ppermute(near, "facet", near_c)
-    mine = moments(band_offset, psf)
-    got = lax.ppermute(mine, "band", CORES)
-    mine, send = combine(mine, got)
-    got = lax.ppermute(send, "band", CHIPS)
+    leaves, stays, send_leaves, send_stays = combine(mine, got)
+    got_leaves = lax.ppermute(send_leaves, "band", CHIPS)
+    got_stays = lax.ppermute(send_stays, "band", CHIPS)
+    sums = dirty_sums(band_offset, dirty)
     near_row, far_row = edges(x, near, far)
     far_row = lax.ppermute(far_row, "facet", far_r)
     near_row = lax.ppermute(near_row, "facet", near_r)
     own = own_rows(x, near, far, table["fc"], table["fr"])
-    y = kernel_spectra(mine, got, table["gc"], table["gr"], table["edge"])
-    sums = dirty_sums(band_offset, dirty)
-    fixed = (y, sums, table["dc"], table["dr"])
-    spec, cross = first(own, near_row, far_row, table["fc"], table["fr"], *fixed[2:], *fixed[:2])
+    fixed = (table["gc"], table["gr"], table["edge"])
+    y = kernel_spectra(leaves, got_leaves, *fixed)
+    rest = (sums, table["dc"], table["dr"])
+    cross = back(MIDDLE, 1, 1, own, y, *rest)
     cross = lax.ppermute(cross, "band", CORES)
-    remote = back(1, 0, spec, *fixed)
-    remote = total(remote, cross)
-    remote = lax.ppermute(remote, "band", CHIPS)
-    cross = back(0, 1, spec, *fixed)
+    middle = back(MIDDLE, 1, 0, own, y, *rest)
+    middle = add(middle, cross)
+    middle = lax.ppermute(middle, "band", CHIPS)
+    spec, cross = first(own, near_row, far_row, table["fc"], table["fr"], y, *rest)
     cross = lax.ppermute(cross, "band", CORES)
-    same = back(0, 0, spec, *fixed)
-    return total(same, cross, remote)[None, None]
+    outer = back(OUTER, 1, 0, spec, y, *rest)
+    outer = add(outer, cross)
+    outer = lax.ppermute(outer, "band", CHIPS)
+    y = kernel_spectra(stays, got_stays, *fixed)
+    cross = back(ALL, 0, 1, spec, y, *rest)
+    cross = lax.ppermute(cross, "band", CORES)
+    same = back(ALL, 0, 0, spec, y, *rest)
+    return last(same, cross, middle, outer)[None, None]
 
 
 def solution(mesh):

time: 42.6 us -> 39.9 us (0.937)
  waiting for transfers between devices: 13.3 us -> 7.62 us
  starting transfers between devices: 15.2 us -> 17.8 us
  Pallas kernels: 13.6 us -> 14.1 us
    ppermute x2 -> x4, starting transfers between devices: 2.08 us -> 4.29 us  [the longest x1 2 us: body(): got_leaves = lax.ppermute(send_leaves, 'band', CHIPS)]
    ppermute x1, waiting for transfers between devices: 1.84 us -> 0.01 us  [body(): got = lax.ppermute(mine, 'band', CORES)]
    ppermute x2 -> x4, waiting for transfers between devices: 7.1 us -> 5.39 us  [the longest x1 3.12 us: body(): outer = lax.ppermute(outer, 'band', CHIPS)]
    ppermute x1, waiting for transfers between devices: 1.54 us -> 0.01 us  [body(): near = lax.ppermute(near, 'facet', near_c)]
    ppermute x1, waiting for transfers between devices: 2.85 us -> 2.21 us  [body(): far = lax.ppermute(far, 'facet', far_c)]
    pallas_call x10 -> x13, Pallas kernels: 10.3 us -> 10.8 us  [the longest x5 4.95 us: back(): pl.pallas_call(functools.partial(product_back, rows, chip, core), in_spec...]
  transfers between devices with their start and end apart: 9 -> 12, of which waited for: 4 -> 3; matrix products, arithmetic and copies ran while one was open for 0% -> 0% of each run, Pallas kernels for 22% -> 30%
where the time goes in v4:
time: 39.9 us; the launch traced here: 39.8 us
  starting transfers between devices  17.8 us (45%)
  Pallas kernels  14.1 us (35%)
  waiting for transfers between devices  7.62 us (19%)
    ppermute x1, starting transfers between devices, body(): far_row = lax.ppermute(far_row, 'facet', far_r)  8.29 us
    pallas_call x5, Pallas kernels, back(): pl.pallas_call(functools.partial(product_back, rows, chip, core), in_spec...  4.95 us
    ppermute x1, waiting for transfers between devices, body(): outer = lax.ppermute(outer, 'band', CHIPS)  3.12 us
    pallas_call x2, Pallas kernels, kernel_spectra(): pl.pallas_call(kernels_kernel, grid=(2,), out_shape=shape(2, NR, NC), in_...  2.58 us
    ppermute x1, waiting for transfers between devices, body(): middle = lax.ppermute(middle, 'band', CHIPS)  2.27 us
    ppermute x1, waiting for transfers between devices, body(): far = lax.ppermute(far, 'facet', far_c)  2.21 us
    ppermute x1, starting transfers between devices, body(): got_leaves = lax.ppermute(send_leaves, 'band', CHIPS)  2 us
    ppermute x1, starting transfers between devices, body(): far = lax.ppermute(far, 'facet', far_c)  1.98 us
  transfers between devices with their start and end apart: 12, of which 3 were waited for; matrix products, arithmetic and copies ran while one was open for 0% of the time, Pallas kernels for 30%

profile of v4, /device:TPU:24, one launch (start us, length us, event | category | flops | bytes accessed | tf_op | source)
XLA Modules:
  0.0 39.8 jit_solution(17527927125898625142)
XLA Ops:
  0.0 1.5 %prepare.1 = (f32[256,256]{1,0:T(8,128)S(1)}, f32[128,128]{1,0:T(8,128)S(1)}, f32[128,128]{1,0:T(8,128)S(1)}, f32[7,136,128]{2,1,0:T(8,128)S(1)}) custom-call(f32[256,256]{1,0:T(8,128)} %bitcast.4, f32[4]{0:T(128)} %off_hbm.3, f32[4,129,1,129]{3,2,1,0:T(1,128)} %bitcast.3), custom_call_target="tpu_custom_call" | custom-call | tf_op jit(solution)/shard_map/prepare/pallas_call | solution.py:180
  1.5 0.1 collective-permute-start.4
  1.6 0.8 %collective-permute-start = (f32[128,128]{1,0:T(8,128)S(1)}, f32[128,128]{1,0:T(8,128)S(1)}, u32[]{:S(2)}, u32[]{:S(2)}) collective-permute-start(f32[128,128]{1,0:T(8,128)S(1)} %get-tuple-element.18), channel_id=1, source_target_pairs={{26,27},{27,26},{28,29},{29,28},{30,31},{31,30},{0,1},{1,0},{2,3},... | collective-permute-start | bytes 196616 | tf_op jit(solution)/shard_map/ppermute | solution.py:482
  2.4 0.0 copy-start.2
  2.4 0.0 copy-start.3
  2.4 2.0 %collective-permute-start.1 = (f32[128,128]{1,0:T(8,128)S(1)}, f32[128,128]{1,0:T(8,128)S(1)}, u32[]{:S(2)}, u32[]{:S(2)}) collective-permute-start(f32[128,128]{1,0:T(8,128)S(1)} %get-tuple-element.19), channel_id=1, source_target_pairs={{27,28},{28,27},{31,0},{0,31},{3,4},{4,3},{7,8},{8,7},{11,12},{12,... | collective-permute-start | bytes 196616 | tf_op jit(solution)/shard_map/ppermute | solution.py:481
  4.4 0.0 collective-permute-done.4.got_ref
  4.4 0.1 combine.1
  4.5 2.0 %collective-permute-start.5 = (f32[2,136,128]{2,1,0:T(8,128)S(1)}, f32[2,136,128]{2,1,0:T(8,128)S(1)}, u32[]{:S(2)}, u32[]{:S(2)}) collective-permute-start(f32[2,136,128]{2,1,0:T(8,128)S(1)} %get-tuple-element.24), channel_id=1, source_target_pairs={{0,64},{64,0},{32,96},{96,32},{1,65},{65,1},{33,97},{97,33},{2,66}... | collective-permute-start | bytes 417800 | tf_op jit(solution)/shard_map/ppermute | solution.py:484
  6.5 0.1 collective-permute-start.6
  6.6 0.0 collective-permute-done.near_ref
  6.6 2.2 %collective-permute-done.1.far_ref = f32[128,128]{1,0:T(8,128)S(1)} collective-permute-done((f32[128,128]{1,0:T(8,128)S(1)}, f32[128,128]{1,0:T(8,128)S(1)}, u32[]{:S(2)}, u32[]{:S(2)}) %collective-permute-start.1) | collective-permute-done | bytes 65568 | tf_op jit(solution)/shard_map/ppermute | solution.py:481
  8.8 0.1 edges.1
  8.9 1.6 %collective-permute-start.2 = (f32[64,384]{1,0:T(8,128)S(1)}, f32[64,384]{1,0:T(8,128)S(1)}, u32[]{:S(2)}, u32[]{:S(2)}) collective-permute-start(f32[64,384]{1,0:T(8,128)S(1)} %get-tuple-element.20), channel_id=1, source_target_pairs={{26,30},{30,26},{27,31},{31,27},{0,4},{4,0},{1,5},{5,1},{2,6},{6,2... | collective-permute-start | bytes 294920 | tf_op jit(solution)/shard_map/ppermute | solution.py:489
  10.5 8.3 %collective-permute-start.3 = (f32[64,384]{1,0:T(8,128)S(1)}, f32[64,384]{1,0:T(8,128)S(1)}, u32[]{:S(2)}, u32[]{:S(2)}) collective-permute-start(f32[64,384]{1,0:T(8,128)S(1)} %get-tuple-element.21), channel_id=1, source_target_pairs={{28,0},{0,28},{29,1},{1,29},{30,2},{2,30},{31,3},{3,31},{4,8},{8,4... | collective-permute-start | bytes 294920 | tf_op jit(solution)/shard_map/ppermute | solution.py:488
  18.7 1.3 %dirty_sums.1.dirty_ref = f32[4,256,256]{2,1,0:T(8,128)S(1)} custom-call(f32[4]{0:T(128)} %off_hbm.3, f32[4,1,256,256]{3,2,1,0:T(8,128)} %dirty_hbm.1), custom_call_target="tpu_custom_call" | custom-call | tf_op jit(solution)/shard_map/dirty_sums/pallas_call | solution.py:335
  20.0 0.0 copy-done.2
  20.0 0.0 copy-done.3
  20.1 0.0 copy-start.4
  20.1 0.0 copy-start.5
  20.1 0.0 copy-start.6
  20.1 0.9 %own_rows.1.own_ref.x_ref = f32[1,384,512]{2,1,0:T(8,128)S(1)} custom-call(f32[256,256]{1,0:T(8,128)S(1)} %get-tuple-element.17.x_ref, f32[128,128]{1,0:T(8,128)S(1)} %collective-permute-done.near_ref, f32[128,128]{1,0:T(8,128)S(1)} %collective-permute-done.1.far_ref, bf16[768,512]{1,0:T(8,128)(2,1)S(1)} %copy-done.2, bf16[384,768]{1,0:T(8,128)(2,1)S(1)} %copy-done.3), custom_call_target="tpu_custom_call" | custom-call | tf_op jit(solution)/shard_map/own_rows/pallas_call | solution.py:241
  21.1 0.0 copy-start
  21.1 0.0 copy-start.1
  21.1 0.0 collective-permute-done.5.got_ref
  21.1 0.0 copy-done.4
  21.1 0.0 copy-done.5
  21.1 0.0 copy-done.6
  21.1 1.3 %kernel_spectra.2.y_ref = f32[2,384,512]{2,1,0:T(8,128)S(1)} custom-call(f32[2,136,128]{2,1,0:T(8,128)S(1)} %get-tuple-element.23.mine_ref, f32[2,136,128]{2,1,0:T(8,128)S(1)} %collective-permute-done.5.got_ref, bf16[256,512]{1,0:T(8,128)(2,1)S(1)} %copy-done.5, bf16[384,288]{1,0:T(8,128)(2,1)S(1)} %copy-done.4, f32[8,512]{1,0:T(8,128)S(1)} %copy-done.6), custom_call_target="tpu_custom_call" | custom-call | tf_op jit(solution)/shard_map/kernel_spectra/pallas_call | solution.py:298
  22.4 0.0 copy-done
  22.4 0.0 copy-done.1
  22.4 0.9 %shard_map.112 = f32[128,256]{1,0:T(8,128)S(1)} custom-call(f32[1,384,512]{2,1,0:T(8,128)S(1)} %own_rows.1.own_ref.x_ref, f32[2,384,512]{2,1,0:T(8,128)S(1)} %kernel_spectra.2.y_ref, f32[4,256,256]{2,1,0:T(8,128)S(1)} %dirty_sums.1.dirty_ref, bf16[1024,256]{1,0:T(8,128)(2,1)S(1)} %copy-done, bf16[256,768]{1,0:T(8,128)(2,1)S(1)} %copy-done.1), custom_call_target="tpu_custom_call" | custom-call | tf_op jit(solution)/shard_map/pallas_call | solution.py:405
  23.4 0.0 collective-permute-done.2.near_ref
  23.4 0.0 collective-permute-done.3.far_ref
  23.4 1.9 %first.1 = (f32[1,384,512]{2,1,0:T(8,128)S(1)}, f32[128,256]{1,0:T(8,128)S(1)}) custom-call(f32[1,384,512]{2,1,0:T(8,128)S(1)} %own_rows.1.own_ref.x_ref, f32[64,384]{1,0:T(8,128)S(1)} %collective-permute-done.2.near_ref, f32[64,384]{1,0:T(8,128)S(1)} %collective-permute-done.3.far_ref, bf16[768,512]{1,0:T(8,128)(2,1)S(1)} %copy-done.2, ...), custom_call_target="tpu_custom_call" | custom-call | tf_op jit(solution)/shard_map/first/pallas_call | solution.py:393
  25.3 0.1 collective-permute-start.10
  25.4 0.5 %collective-permute-start.8 = (f32[128,256]{1,0:T(8,128)S(1)}, f32[128,256]{1,0:T(8,128)S(1)}, u32[]{:S(2)}, u32[]{:S(2)}) collective-permute-start(f32[128,256]{1,0:T(8,128)S(1)} %shard_map.112), channel_id=1, source_target_pairs={{0,32},{32,0},{64,96},{96,64},{1,33},{33,1},{65,97},{97,65},{2,34}... | collective-permute-start | bytes 393224 | tf_op jit(solution)/shard_map/ppermute | solution.py:495
  25.9 0.0 collective-permute-done.6.got_ref
  25.9 1.3 %kernel_spectra.3.y_ref = f32[2,384,512]{2,1,0:T(8,128)S(1)} custom-call(f32[2,136,128]{2,1,0:T(8,128)S(1)} %get-tuple-element.26.mine_ref, f32[2,136,128]{2,1,0:T(8,128)S(1)} %collective-permute-done.6.got_ref, bf16[256,512]{1,0:T(8,128)(2,1)S(1)} %copy-done.5, bf16[384,288]{1,0:T(8,128)(2,1)S(1)} %copy-done.4, f32[8,512]{1,0:T(8,128)S(1)} %copy-done.6), custom_call_target="tpu_custom_call" | custom-call | tf_op jit(solution)/shard_map/kernel_spectra/pallas_call | solution.py:298
  27.1 1.1 %shard_map.110 = f32[256,256]{1,0:T(8,128)S(1)} custom-call(f32[1,384,512]{2,1,0:T(8,128)S(1)} %get-tuple-element.25.x_ref, f32[2,384,512]{2,1,0:T(8,128)S(1)} %kernel_spectra.3.y_ref, f32[4,256,256]{2,1,0:T(8,128)S(1)} %dirty_sums.1.dirty_ref, bf16[1024,256]{1,0:T(8,128)(2,1)S(1)} %copy-done, bf16[256,768]{1,0:T(8,128)(2,1)S(1)} %copy-done.1), custom_call_target="tpu_custom_call" | custom-call | tf_op jit(solution)/shard_map/pallas_call | solution.py:405
  28.3 0.2 collective-permute-start.7
  28.4 0.9 %shard_map.113.a_ref = f32[128,256]{1,0:T(8,128)S(1)} custom-call(f32[1,384,512]{2,1,0:T(8,128)S(1)} %get-tuple-element.25.x_ref, f32[2,384,512]{2,1,0:T(8,128)S(1)} %kernel_spectra.2.y_ref, f32[4,256,256]{2,1,0:T(8,128)S(1)} %dirty_sums.1.dirty_ref, bf16[1024,256]{1,0:T(8,128)(2,1)S(1)} %copy-done, bf16[256,768]{1,0:T(8,128)(2,1)S(1)} %copy-done.1), custom_call_target="tpu_custom_call" | custom-call | tf_op jit(solution)/shard_map/pallas_call | solution.py:405
  29.4 0.9 %shard_map.111.a_ref = f32[128,256]{1,0:T(8,128)S(1)} custom-call(f32[1,384,512]{2,1,0:T(8,128)S(1)} %own_rows.1.own_ref.x_ref, f32[2,384,512]{2,1,0:T(8,128)S(1)} %kernel_spectra.2.y_ref, f32[4,256,256]{2,1,0:T(8,128)S(1)} %dirty_sums.1.dirty_ref, bf16[1024,256]{1,0:T(8,128)(2,1)S(1)} %copy-done, bf16[256,768]{1,0:T(8,128)(2,1)S(1)} %copy-done.1), custom_call_target="tpu_custom_call" | custom-call | tf_op jit(solution)/shard_map/pallas_call | solution.py:405
  30.3 0.0 collective-permute-done.10.b_ref
  30.3 1.1 %collective-permute-start.11 = (f32[128,256]{1,0:T(8,128)S(1)}, f32[128,256]{1,0:T(8,128)S(1)}, u32[]{:S(2)}, u32[]{:S(2)}) collective-permute-start(f32[128,256]{1,0:T(8,128)S(1)} %add.3), channel_id=1, source_target_pairs={{0,64},{64,0},{32,96},{96,32},{1,65},{65,1},{33,97},{97,33},{2,66}... | collective-permute-start | bytes 393224 | tf_op jit(solution)/shard_map/ppermute | solution.py:503
  31.4 0.0 collective-permute-done.8.b_ref
  31.4 1.1 %collective-permute-start.9 = (f32[128,256]{1,0:T(8,128)S(1)}, f32[128,256]{1,0:T(8,128)S(1)}, u32[]{:S(2)}, u32[]{:S(2)}) collective-permute-start(f32[128,256]{1,0:T(8,128)S(1)} %add.2), channel_id=1, source_target_pairs={{0,64},{64,0},{32,96},{96,32},{1,65},{65,1},{33,97},{97,33},{2,66}... | collective-permute-start | bytes 393224 | tf_op jit(solution)/shard_map/ppermute | solution.py:498
  32.5 1.1 %shard_map.109.a_ref = f32[256,256]{1,0:T(8,128)S(1)} custom-call(f32[1,384,512]{2,1,0:T(8,128)S(1)} %get-tuple-element.25.x_ref, f32[2,384,512]{2,1,0:T(8,128)S(1)} %kernel_spectra.3.y_ref, f32[4,256,256]{2,1,0:T(8,128)S(1)} %dirty_sums.1.dirty_ref, bf16[1024,256]{1,0:T(8,128)(2,1)S(1)} %copy-done, bf16[256,768]{1,0:T(8,128)(2,1)S(1)} %copy-done.1), custom_call_target="tpu_custom_call" | custom-call | tf_op jit(solution)/shard_map/pallas_call | solution.py:405
  33.6 3.1 %collective-permute-done.11.outer_ref = f32[128,256]{1,0:T(8,128)S(1)} collective-permute-done((f32[128,256]{1,0:T(8,128)S(1)}, f32[128,256]{1,0:T(8,128)S(1)}, u32[]{:S(2)}, u32[]{:S(2)}) %collective-permute-start.11) | collective-permute-done | bytes 131104 | tf_op jit(solution)/shard_map/ppermute | solution.py:503
  36.8 2.3 %collective-permute-done.9.middle_ref = f32[128,256]{1,0:T(8,128)S(1)} collective-permute-done((f32[128,256]{1,0:T(8,128)S(1)}, f32[128,256]{1,0:T(8,128)S(1)}, u32[]{:S(2)}, u32[]{:S(2)}) %collective-permute-start.9) | collective-permute-done | bytes 131104 | tf_op jit(solution)/shard_map/ppermute | solution.py:498
  39.0 0.0 collective-permute-done.7.b_ref
  39.0 0.7 %last.1 = f32[256,256]{1,0:T(8,128)} custom-call(f32[256,256]{1,0:T(8,128)S(1)} %shard_map.109.a_ref, f32[256,256]{1,0:T(8,128)S(1)} %collective-permute-done.7.b_ref, f32[128,256]{1,0:T(8,128)S(1)} %collective-permute-done.9.middle_ref, f32[128,256]{1,0:T(8,128)S(1)} %collective-permute-done.11.outer_ref), custom_call_target="tpu_custom_call" | custom-call | tf_op jit(solution)/shard_map/last/pallas_call | solution.py:440
  (2 shorter events, 0.0 us)
Async XLA Ops:
  1.5 2.9 %collective-permute-start.4 = (f32[7,136,128]{2,1,0:T(8,128)S(1)}, f32[7,136,128]{2,1,0:T(8,128)S(1)}, u32[]{:S(2)}, u32[]{:S(2)}) collective-permute-start(f32[7,136,128]{2,1,0:T(8,128)S(1)} %get-tuple-element.22.mine_ref), channel_id=1, source_target_pairs={{0,32},{32,0},{64,96},{96,64},{1,33},{33,1},{65,97},{97,65},{2,34}... | collective-permute-start | bytes 1462280 | tf_op jit(solution)/shard_map/ppermute | solution.py:480
  1.6 5.0 %collective-permute-start = (f32[128,128]{1,0:T(8,128)S(1)}, f32[128,128]{1,0:T(8,128)S(1)}, u32[]{:S(2)}, u32[]{:S(2)}) collective-permute-start(f32[128,128]{1,0:T(8,128)S(1)} %get-tuple-element.18), channel_id=1, source_target_pairs={{26,27},{27,26},{28,29},{29,28},{30,31},{31,30},{0,1},{1,0},{2,3},... | collective-permute-start | bytes 196616 | tf_op jit(solution)/shard_map/ppermute | solution.py:482
  2.4 17.6 %copy-start.2 = (bf16[768,512]{1,0:T(8,128)(2,1)S(1)}, bf16[768,512]{1,0:T(8,128)(2,1)}, u32[]{:S(2)}) copy-start(bf16[768,512]{1,0:T(8,128)(2,1)} %constant.14.clone.fc_ref) | copy-start | bytes 2359300
  2.4 17.6 %copy-start.3 = (bf16[384,768]{1,0:T(8,128)(2,1)S(1)}, bf16[384,768]{1,0:T(8,128)(2,1)}, u32[]{:S(2)}) copy-start(bf16[384,768]{1,0:T(8,128)(2,1)} %constant.15.clone.fr_ref) | copy-start | bytes 1769476
  2.4 6.4 %collective-permute-start.1 = (f32[128,128]{1,0:T(8,128)S(1)}, f32[128,128]{1,0:T(8,128)S(1)}, u32[]{:S(2)}, u32[]{:S(2)}) collective-permute-start(f32[128,128]{1,0:T(8,128)S(1)} %get-tuple-element.19), channel_id=1, source_target_pairs={{27,28},{28,27},{31,0},{0,31},{3,4},{4,3},{7,8},{8,7},{11,12},{12,... | collective-permute-start | bytes 196616 | tf_op jit(solution)/shard_map/ppermute | solution.py:481
  4.5 16.6 %collective-permute-start.5 = (f32[2,136,128]{2,1,0:T(8,128)S(1)}, f32[2,136,128]{2,1,0:T(8,128)S(1)}, u32[]{:S(2)}, u32[]{:S(2)}) collective-permute-start(f32[2,136,128]{2,1,0:T(8,128)S(1)} %get-tuple-element.24), channel_id=1, source_target_pairs={{0,64},{64,0},{32,96},{96,32},{1,65},{65,1},{33,97},{97,33},{2,66}... | collective-permute-start | bytes 417800 | tf_op jit(solution)/shard_map/ppermute | solution.py:484
  6.5 19.4 %collective-permute-start.6 = (f32[2,136,128]{2,1,0:T(8,128)S(1)}, f32[2,136,128]{2,1,0:T(8,128)S(1)}, u32[]{:S(2)}, u32[]{:S(2)}) collective-permute-start(f32[2,136,128]{2,1,0:T(8,128)S(1)} %get-tuple-element.27), channel_id=1, source_target_pairs={{0,64},{64,0},{32,96},{96,32},{1,65},{65,1},{33,97},{97,33},{2,66}... | collective-permute-start | bytes 417800 | tf_op jit(solution)/shard_map/ppermute | solution.py:485
  8.9 14.5 %collective-permute-start.2 = (f32[64,384]{1,0:T(8,128)S(1)}, f32[64,384]{1,0:T(8,128)S(1)}, u32[]{:S(2)}, u32[]{:S(2)}) collective-permute-start(f32[64,384]{1,0:T(8,128)S(1)} %get-tuple-element.20), channel_id=1, source_target_pairs={{26,30},{30,26},{27,31},{31,27},{0,4},{4,0},{1,5},{5,1},{2,6},{6,2... | collective-permute-start | bytes 294920 | tf_op jit(solution)/shard_map/ppermute | solution.py:489
  10.5 12.9 %collective-permute-start.3 = (f32[64,384]{1,0:T(8,128)S(1)}, f32[64,384]{1,0:T(8,128)S(1)}, u32[]{:S(2)}, u32[]{:S(2)}) collective-permute-start(f32[64,384]{1,0:T(8,128)S(1)} %get-tuple-element.21), channel_id=1, source_target_pairs={{28,0},{0,28},{29,1},{1,29},{30,2},{2,30},{31,3},{3,31},{4,8},{8,4... | collective-permute-start | bytes 294920 | tf_op jit(solution)/shard_map/ppermute | solution.py:488
  20.1 1.0 %copy-start.4 = (bf16[384,288]{1,0:T(8,128)(2,1)S(1)}, bf16[384,288]{1,0:T(8,128)(2,1)}, u32[]{:S(2)}) copy-start(bf16[384,288]{1,0:T(8,128)(2,1)} %constant.17.clone.gr_ref) | copy-start | bytes 663556
  20.1 1.0 %copy-start.5 = (bf16[256,512]{1,0:T(8,128)(2,1)S(1)}, bf16[256,512]{1,0:T(8,128)(2,1)}, u32[]{:S(2)}) copy-start(bf16[256,512]{1,0:T(8,128)(2,1)} %constant.16.clone.gc_ref) | copy-start | bytes 786436
  20.1 1.0 %copy-start.6 = (f32[8,512]{1,0:T(8,128)S(1)}, f32[8,512]{1,0:T(8,128)}, u32[]{:S(2)}) copy-start(f32[8,512]{1,0:T(8,128)} %constant.20.clone.edge_ref) | copy-start | bytes 49156
  21.1 1.4 %copy-start = (bf16[1024,256]{1,0:T(8,128)(2,1)S(1)}, bf16[1024,256]{1,0:T(8,128)(2,1)}, u32[]{:S(2)}) copy-start(bf16[1024,256]{1,0:T(8,128)(2,1)} %constant.18.clone.dc_ref) | copy-start | bytes 1572868
  21.1 1.4 %copy-start.1 = (bf16[256,768]{1,0:T(8,128)(2,1)S(1)}, bf16[256,768]{1,0:T(8,128)(2,1)}, u32[]{:S(2)}) copy-start(bf16[256,768]{1,0:T(8,128)(2,1)} %constant.19.clone.dr_ref) | copy-start | bytes 1179652
  25.3 5.0 %collective-permute-start.10 = (f32[128,256]{1,0:T(8,128)S(1)}, f32[128,256]{1,0:T(8,128)S(1)}, u32[]{:S(2)}, u32[]{:S(2)}) collective-permute-start(f32[128,256]{1,0:T(8,128)S(1)} %get-tuple-element.28), channel_id=1, source_target_pairs={{0,32},{32,0},{64,96},{96,64},{1,33},{33,1},{65,97},{97,65},{2,34}... | collective-permute-start | bytes 393224 | tf_op jit(solution)/shard_map/ppermute | solution.py:500
  25.4 6.0 %collective-permute-start.8 = (f32[128,256]{1,0:T(8,128)S(1)}, f32[128,256]{1,0:T(8,128)S(1)}, u32[]{:S(2)}, u32[]{:S(2)}) collective-permute-start(f32[128,256]{1,0:T(8,128)S(1)} %shard_map.112), channel_id=1, source_target_pairs={{0,32},{32,0},{64,96},{96,64},{1,33},{33,1},{65,97},{97,65},{2,34}... | collective-permute-start | bytes 393224 | tf_op jit(solution)/shard_map/ppermute | solution.py:495
  28.3 10.8 %collective-permute-start.7 = (f32[256,256]{1,0:T(8,128)S(1)}, f32[256,256]{1,0:T(8,128)S(1)}, u32[]{:S(2)}, u32[]{:S(2)}) collective-permute-start(f32[256,256]{1,0:T(8,128)S(1)} %shard_map.110), channel_id=1, source_target_pairs={{0,32},{32,0},{64,96},{96,64},{1,33},{33,1},{65,97},{97,65},{2,34}... | collective-permute-start | bytes 786440 | tf_op jit(solution)/shard_map/ppermute | solution.py:506
  30.3 6.5 %collective-permute-start.11 = (f32[128,256]{1,0:T(8,128)S(1)}, f32[128,256]{1,0:T(8,128)S(1)}, u32[]{:S(2)}, u32[]{:S(2)}) collective-permute-start(f32[128,256]{1,0:T(8,128)S(1)} %add.3), channel_id=1, source_target_pairs={{0,64},{64,0},{32,96},{96,32},{1,65},{65,1},{33,97},{97,33},{2,66}... | collective-permute-start | bytes 393224 | tf_op jit(solution)/shard_map/ppermute | solution.py:503
  31.4 7.6 %collective-permute-start.9 = (f32[128,256]{1,0:T(8,128)S(1)}, f32[128,256]{1,0:T(8,128)S(1)}, u32[]{:S(2)}, u32[]{:S(2)}) collective-permute-start(f32[128,256]{1,0:T(8,128)S(1)} %add.2), channel_id=1, source_target_pairs={{0,64},{64,0},{32,96},{96,32},{1,65},{65,1},{33,97},{97,33},{2,66}... | collective-permute-start | bytes 393224 | tf_op jit(solution)/shard_map/ppermute | solution.py:498
